TPU v7x, 128 devices: a whole 4x4x4 slice. The times are simulated.
128 devices in a mesh: gx: 8 (over z, core), gy: 16 (over x, y).
Axes of the slice: x: 4, y: 4, z: 4, core: 2. Of those that a mesh axis runs over, the one named last changes fastest.
Arguments:
- state_prev: float32 [256, 128, 1024], P('gy', None, 'gx'), may hold values from -60 to 60
- diffusivity: float32 [256, 128, 1024], P('gy', None, 'gx'), may hold values from 0.5 to 4
- vapour: float32 [256, 128, 1024], P('gy', None, 'gx'), may hold values from 0.01 to 0.1
- cos_zenith: float32 [256, 1024], P('gy', 'gx'), may hold values from 0.1 to 1
- albedo: float32 [256, 1024], P('gy', 'gx'), may hold values from 0.05 to 0.8
- absorption: float32 [128, 112], replicated, may hold values from 0.005 to 1
- solar_weight: float32 [112], replicated, may hold values from 0.002 to 0.02
- day_mask: int32 [2048], P(('gx', 'gy')), may hold values from 0 to 1, as said below
Outputs:
- state_next: float32 [256, 128, 1024], P('gy', None, 'gx')
- residual: float32 [256, 128, 1024], P('gy', None, 'gx')
- net_flux: float32 [256, 128, 1024], P('gy', None, 'gx')
Inputs may be any that keep to these rules, and one draw needn't show every extreme that they name: `day_mask`: exactly half of the 2048 entries are 1, and some device holds only sunlit blocks.
All inputs are finite; a program needn't handle non-finite values.
Results may differ from a plain program's by a relative error of at most 0.00015.
Values sent between devices are 32-bit elements; how exact they have to be, the bound alone decides.
No kernel may reach another device: no remote copies, remote signals or barrier semaphores. Data moves between devices by JAX's collectives and lax.ppermute only.
A program may use at most 128 MiB of HBM per device.

v0:
```python
import jax
import jax.numpy as jnp
from jax import lax
from jax.sharding import Mesh
from jax.sharding import PartitionSpec as P

ITERS = 5
GX = ("gx_0", "gx_1")
GY = ("gy_0", "gy_1")
GX_GY = ("gx_0", "gx_1", "gy_0", "gy_1")


def padded(array, sides, width, wrap):
    for axis, dim in sides:
        devices, length = (lax.axis_size(axis), array.shape[dim])
        up = [(i, (i + 1) % devices) for i in range(devices if wrap else devices - 1)]
        down = [(j, i) for i, j in up]
        last = lax.slice_in_dim(array, length - width, length, axis=dim)
        first = lax.slice_in_dim(array, 0, width, axis=dim)
        before = lax.ppermute(last, axis, up)
        after = lax.ppermute(first, axis, down)
        array = jnp.concatenate([before, array, after], axis=dim)
    return array


def one_axis_at_a_time(array, axes):
    for axis in axes:
        array = lax.psum(array, axis)
    return array


def in_order(blocks, dim):
    blocks = jnp.moveaxis(blocks, 0, dim)
    shape = blocks.shape
    return blocks.reshape(*shape[:dim], shape[dim] * shape[dim + 1], *shape[dim + 2 :])


def stacked_from(array, axes, sequence):
    blocks = array
    for k in sequence:
        blocks = lax.all_gather(blocks, axes[k])
    done = sequence[::-1]
    back = [done.index(k) for k in range(len(axes))]
    blocks = blocks.transpose(*back, *range(len(axes), blocks.ndim))
    return blocks.reshape(-1, *array.shape)


def gathered_by_axis(array, axes, sequence, dim):
    return in_order(stacked_from(array, axes, sequence), dim)


def longitude_edges(values):
    return padded(values, ((GX, 2),), 1, True)


def latitude_edges(values):
    return padded(values, ((GY, 0),), 1, False)


def face_terms(diffusivity):
    widened = longitude_edges(diffusivity)
    extended = latitude_edges(diffusivity)
    east_face = jnp.sqrt(diffusivity * widened[:, :, 2:])
    west_face = jnp.sqrt(diffusivity * widened[:, :, :-2])
    north_face = jnp.sqrt(diffusivity * extended[2:])
    south_face = jnp.sqrt(diffusivity * extended[:-2])
    level_face = jnp.sqrt(diffusivity[:, 1:] * diffusivity[:, :-1])
    return (east_face, west_face, north_face, south_face, level_face)


def operate(values, conductances):
    east_face, west_face, north_face, south_face, level_face = conductances
    widened = longitude_edges(values)
    extended = latitude_edges(values)
    applied = (
        values
        + east_face * (values - widened[:, :, 2:])
        + west_face * (values - widened[:, :, :-2])
    )
    applied = applied + north_face * (values - extended[2:]) + south_face * (values - extended[:-2])
    vertical = level_face * (values[:, 1:] - values[:, :-1])
    padding = jnp.zeros_like(values[:, :1])
    return (
        applied - jnp.concatenate([vertical, padding], 1) + jnp.concatenate([padding, vertical], 1)
    )


def squares(residual):
    return one_axis_at_a_time(jnp.sum(residual * residual), GX_GY)


def radiate(layer_amount, sunlight, triangle, absorption, solar_weight):
    levels = layer_amount.shape[0]
    columns = layer_amount.shape[1]
    gpoints = absorption.shape[1]
    thickness = absorption[:, :, None] * layer_amount[:, None, :]
    cumulative = jnp.dot(
        triangle,
        thickness.reshape(levels, gpoints * columns),
        precision=lax.Precision.HIGHEST,
        preferred_element_type=jnp.float32,
    )
    cumulative = cumulative.reshape(levels, gpoints, columns)
    cosine = sunlight[0]
    surface = sunlight[1]
    downward = cosine * jnp.exp(-cumulative / cosine)
    upward = surface * downward[-1] * jnp.exp(-1.66 * (cumulative[-1] - cumulative))
    return jnp.einsum("lgc,g->lc", downward - upward, solar_weight, precision=lax.Precision.HIGHEST)


def body(state_prev, diffusivity, vapour, cos_zenith, albedo, absorption, solar_weight, day_mask):
    conductances = face_terms(diffusivity)
    state_next = state_prev
    residual = state_prev - operate(state_prev, conductances)
    direction = residual
    current = squares(residual)
    for iteration in range(ITERS):
        applied = operate(direction, conductances)
        curvature_sum = one_axis_at_a_time(jnp.sum(direction * applied), GX_GY)
        step_size = current / curvature_sum
        state_next = state_next + step_size * direction
        residual = residual - step_size * applied
        following = squares(residual)
        direction = residual + following / current * direction
        current = following
    optical = vapour * (1.0 + 0.5 * jnp.tanh(state_prev))
    sunlight = jnp.stack([cos_zenith, albedo], 1)
    levels = optical.shape[1]
    triangle = (
        lax.broadcasted_iota(jnp.int32, (levels, levels), 0)
        >= lax.broadcasted_iota(jnp.int32, (levels, levels), 1)
    ).astype(jnp.float32)

    def slab_flux(inputs):
        return radiate(inputs[0], inputs[1], triangle, absorption, solar_weight)

    lit_blocks = day_mask.astype(jnp.float32)[:, None, None]
    whole_mask = gathered_by_axis(day_mask, GX_GY, (0, 2, 3, 1), 0)
    devices = lax.axis_size(GX) * lax.axis_size(GY)
    blocks = day_mask.shape[0]
    width = optical.shape[2]
    capacity = blocks * width // devices
    working = blocks * width // 2
    myself = lax.axis_index(GX) * lax.axis_size(GY) + lax.axis_index(GY)
    per_device = jnp.sum(whole_mask.reshape(devices, blocks), 1)
    ends = jnp.cumsum(per_device) * width
    starts = ends - per_device * width
    my_start = jnp.take(starts, myself)
    my_end = jnp.take(ends, myself)
    own_rank = jnp.cumsum(day_mask) - 1
    peer_ids = lax.broadcasted_iota(jnp.int32, (devices, capacity), 0)
    slot_ids = lax.broadcasted_iota(jnp.int32, (devices, capacity), 1)
    first = my_start + (peer_ids - my_start) % devices
    wanted = first + slot_ids * devices
    valid_send = (wanted < my_end).astype(jnp.float32)
    offset = wanted - my_start
    rank_needed = offset // width
    row_hits = (own_rank[None, None, :] == rank_needed[:, :, None]) & (day_mask[None, None, :] == 1)
    row_ids = lax.broadcasted_iota(jnp.int32, (1, 1, blocks), 2)
    row_of = jnp.sum(jnp.where(row_hits, row_ids, 0), 2)
    flat_send = jnp.clip(row_of * width + offset % width, 0, blocks * width - 1)
    packed = jnp.concatenate([optical, sunlight], 1)
    packed = jnp.transpose(packed, (1, 0, 2)).reshape(levels + 2, blocks * width)
    outgoing = jnp.take(packed, flat_send.reshape(-1), 1).reshape(levels + 2, devices, capacity)
    outgoing = jnp.transpose(outgoing * valid_send[None], (1, 0, 2))
    arrived = lax.all_to_all(outgoing, GX_GY, split_axis=0, concat_axis=0, tiled=True)
    work_ids = lax.broadcasted_iota(jnp.int32, (working,), 0)
    global_ids = work_ids * devices + myself
    source = jnp.sum((ends[None, :] <= global_ids[:, None]).astype(jnp.int32), 1)
    source = jnp.clip(source, 0, devices - 1)
    source_start = jnp.take(starts, source)
    source_first = source_start + (myself - source_start) % devices
    flat_work = jnp.clip(
        source * capacity + (global_ids - source_first) // devices, 0, devices * capacity - 1
    )
    arrived_flat = jnp.transpose(arrived, (1, 0, 2)).reshape(levels + 2, devices * capacity)
    work = jnp.take(arrived_flat, flat_work, 1).reshape(levels + 2, working // width, width)
    work = jnp.transpose(work, (1, 0, 2))
    fluxes = lax.map(slab_flux, (work[:, :levels], work[:, levels:]))
    fluxes = jnp.transpose(fluxes, (1, 0, 2)).reshape(levels, working)
    peer_start = starts[:, None]
    back_ids = peer_start + (myself - peer_start) % devices + slot_ids * devices
    valid_back = (back_ids < ends[:, None]).astype(jnp.float32)
    back_slot = jnp.clip((back_ids - myself) // devices, 0, working - 1)
    returning = jnp.take(fluxes, back_slot.reshape(-1), 1).reshape(levels, devices, capacity)
    returning = jnp.transpose(returning * valid_back[None], (1, 0, 2))
    came_back = lax.all_to_all(returning, GX_GY, split_axis=0, concat_axis=0, tiled=True)
    column_ids = lax.broadcasted_iota(jnp.int32, (blocks, width), 1)
    own_ids = my_start + jnp.clip(own_rank, 0, blocks - 1)[:, None] * width + column_ids
    home_peer = own_ids % devices
    home_first = my_start + (home_peer - my_start) % devices
    flat_home = jnp.clip(
        home_peer * capacity + (own_ids - home_first) // devices, 0, devices * capacity - 1
    )
    back_flat = jnp.transpose(came_back, (1, 0, 2)).reshape(levels, devices * capacity)
    placed = jnp.take(back_flat, flat_home.reshape(-1), 1).reshape(levels, blocks, width)
    net_flux = jnp.transpose(placed, (1, 0, 2)) * lit_blocks
    return (state_next, residual, net_flux)


def solution(mesh):
    torus = Mesh(mesh.devices.reshape(4, 2, 4, 4), ("gx_0", "gx_1", "gy_0", "gy_1"))
    in_specs = (
        P(GY, None, GX),
        P(GY, None, GX),
        P(GY, None, GX),
        P(GY, GX),
        P(GY, GX),
        P(),
        P(),
        P(GX_GY),
    )
    out_specs = (P(GY, None, GX), P(GY, None, GX), P(GY, None, GX))
    return jax.shard_map(body, mesh=torus, in_specs=in_specs, out_specs=out_specs, check_vma=False)
```

profile of v0, /device:TPU:100, one launch (start us, length us, event | category | flops | bytes accessed | tf_op | source)
XLA Modules:
  0.0 896.5 jit_solution(10297394391904766983)
XLA Ops:
  28.5 10.1 %all-gather.4 = s32[4,4,16]{2,1,0:T(4,128)S(1)} all-gather(s32[1,4,16]{2,1,0:T(4,128)S(1)} %reshape.966), channel_id=3, replica_groups=mesh['gx_0'=4,'gx_1'=2,'gy_0'=4,'gy_1'=4] {'gy_0'}, dimensions={0}, use_global_device_ids=true | all-gather | bytes 1280 | tf_op jit(solution)/shard_map/all_gather | solution.py:41
  38.6 11.9 %all-gather.2 = s32[16,4,16]{2,1,0:T(4,128)S(1)} all-gather(s32[4,4,16]{2,1,0:T(4,128)S(1)} %all-gather.4), channel_id=4, replica_groups=mesh['gx_0'=4,'gx_1'=2,'gy_0'=4,'gy_1'=4] {'gy_1'}, dimensions={0}, use_global_device_ids=true | all-gather | bytes 5120 | tf_op jit(solution)/shard_map/all_gather | solution.py:41
  98.7 10.7 %all-reduce.15 = (f32[]{:T(128)}, f32[]{:T(128)}) all-reduce(f32[]{:T(128)} %get-tuple-element.87, f32[]{:T(128)} %get-tuple-element.86), channel_id=1, replica_groups=mesh['gx_0'=4,'gx_1'=2,'gy_0'=4,'gy_1'=4] {'gx_0'}, use_global_device_ids=true, to_apply=%region_1.0 | all-reduce | flops 2 | bytes 16 | tf_op jit(solution)/shard_map/psum | solution.py:28
  120.6 10.1 %all-reduce.13 = (f32[]{:T(128)}, f32[]{:T(128)}) all-reduce(f32[]{:T(128)} %get-tuple-element.102, f32[]{:T(128)} %get-tuple-element.103), channel_id=1, replica_groups=mesh['gx_0'=4,'gx_1'=2,'gy_0'=4,'gy_1'=4] {'gy_1'}, use_global_device_ids=true, to_apply=%region_4.0 | all-reduce | flops 2 | bytes 16 | tf_op jit(solution)/shard_map/psum | solution.py:28
  134.2 9.3 %psum.288 = f32[]{:T(128)} all-reduce(f32[]{:T(128)} %multiply_reduce_fusion.7), channel_id=1, replica_groups=mesh['gx_0'=4,'gx_1'=2,'gy_0'=4,'gy_1'=4] {'gx_0'}, use_global_device_ids=true, to_apply=%region_11.0 | all-reduce | flops 1 | bytes 8 | tf_op jit(solution)/shard_map/psum | solution.py:28
  186.2 10.7 %psum.292 = f32[]{:T(128)} all-reduce(f32[]{:T(128)} %get-tuple-element.122), channel_id=1, replica_groups=mesh['gx_0'=4,'gx_1'=2,'gy_0'=4,'gy_1'=4] {'gx_0'}, use_global_device_ids=true, to_apply=%region_16.0 | all-reduce | flops 1 | bytes 8 | tf_op jit(solution)/shard_map/psum | solution.py:28
  200.1 9.7 %psum.294 = f32[]{:T(128)} all-reduce(f32[]{:T(128)} %psum.293), channel_id=1, replica_groups=mesh['gx_0'=4,'gx_1'=2,'gy_0'=4,'gy_1'=4] {'gy_0'}, use_global_device_ids=true, to_apply=%region_18.0 | all-reduce | flops 1 | bytes 8 | tf_op jit(solution)/shard_map/psum | solution.py:28
  209.8 10.1 %gather_fusion.1 = f32[2048,130]{1,0:T(8,128)} fusion(f32[130,2048]{0,1:T(8,128)} %bitcast.117, s32[2048]{0:T(1024)S(1)} %broadcast_clamp_fusion.2), kind=kCustom, calls=%fused_computation.1 | custom fusion | bytes 2138112 | tf_op jit(solution)/shard_map/jit(_take)/gather | solution.py:164
  233.6 9.4 %psum.296 = f32[]{:T(128)} all-reduce(f32[]{:T(128)} %get-tuple-element.120), channel_id=1, replica_groups=mesh['gx_0'=4,'gx_1'=2,'gy_0'=4,'gy_1'=4] {'gx_0'}, use_global_device_ids=true, to_apply=%region_21.0 | all-reduce | flops 1 | bytes 8 | tf_op jit(solution)/shard_map/psum | solution.py:28
  249.1 9.4 %all-to-all-start = ((f32[128,130,16]{1,2,0:T(8,128)}), f32[128,130,16]{1,2,0:T(8,128)}, u32[]{:S(2)}, u32[]{:S(2)}) async-start(f32[128,130,16]{1,2,0:T(8,128)} %multiply_bitcast_fusion), calls=%async_computation | async-start | bytes 4194304 | tf_op jit(solution)/shard_map/all_to_all | solution.py:166
  258.5 25.9 %psum.298 = f32[]{:T(128)} all-reduce(f32[]{:T(128)} %psum.297), channel_id=1, replica_groups=mesh['gx_0'=4,'gx_1'=2,'gy_0'=4,'gy_1'=4] {'gy_0'}, use_global_device_ids=true, to_apply=%region_23.0 | all-reduce | flops 1 | bytes 8 | tf_op jit(solution)/shard_map/psum | solution.py:28
  285.0 11.6 %psum.299 = f32[]{:T(128)} all-reduce(f32[]{:T(128)} %psum.298), channel_id=1, replica_groups=mesh['gx_0'=4,'gx_1'=2,'gy_0'=4,'gy_1'=4] {'gy_1'}, use_global_device_ids=true, to_apply=%region_24.0 | all-reduce | flops 1 | bytes 8 | tf_op jit(solution)/shard_map/psum | solution.py:28
  326.0 9.2 %psum.302 = f32[]{:T(128)} all-reduce(f32[]{:T(128)} %psum.301), channel_id=1, replica_groups=mesh['gx_0'=4,'gx_1'=2,'gy_0'=4,'gy_1'=4] {'gy_0'}, use_global_device_ids=true, to_apply=%region_28.0 | all-reduce | flops 1 | bytes 8 | tf_op jit(solution)/shard_map/psum | solution.py:28
  335.3 9.9 %psum.303 = f32[]{:T(128)} all-reduce(f32[]{:T(128)} %psum.302), channel_id=1, replica_groups=mesh['gx_0'=4,'gx_1'=2,'gy_0'=4,'gy_1'=4] {'gy_1'}, use_global_device_ids=true, to_apply=%region_29.0 | all-reduce | flops 1 | bytes 8 | tf_op jit(solution)/shard_map/psum | solution.py:28
  349.5 10.6 %psum.304 = f32[]{:T(128)} all-reduce(f32[]{:T(128)} %get-tuple-element.116), channel_id=1, replica_groups=mesh['gx_0'=4,'gx_1'=2,'gy_0'=4,'gy_1'=4] {'gx_0'}, use_global_device_ids=true, to_apply=%region_31.0 | all-reduce | flops 1 | bytes 8 | tf_op jit(solution)/shard_map/psum | solution.py:28
  363.0 9.9 %psum.306 = f32[]{:T(128)} all-reduce(f32[]{:T(128)} %psum.305), channel_id=1, replica_groups=mesh['gx_0'=4,'gx_1'=2,'gy_0'=4,'gy_1'=4] {'gy_0'}, use_global_device_ids=true, to_apply=%region_33.0 | all-reduce | flops 1 | bytes 8 | tf_op jit(solution)/shard_map/psum | solution.py:28
  406.3 9.6 %psum.308 = f32[]{:T(128)} all-reduce(f32[]{:T(128)} %get-tuple-element.114), channel_id=1, replica_groups=mesh['gx_0'=4,'gx_1'=2,'gy_0'=4,'gy_1'=4] {'gx_0'}, use_global_device_ids=true, to_apply=%region_36.0 | all-reduce | flops 1 | bytes 8 | tf_op jit(solution)/shard_map/psum | solution.py:28
  419.1 9.0 %psum.310 = f32[]{:T(128)} all-reduce(f32[]{:T(128)} %psum.309), channel_id=1, replica_groups=mesh['gx_0'=4,'gx_1'=2,'gy_0'=4,'gy_1'=4] {'gy_0'}, use_global_device_ids=true, to_apply=%region_38.0 | all-reduce | flops 1 | bytes 8 | tf_op jit(solution)/shard_map/psum | solution.py:28
  428.1 8.9 psum.311
  441.6 10.4 %psum.312 = f32[]{:T(128)} all-reduce(f32[]{:T(128)} %get-tuple-element.112), channel_id=1, replica_groups=mesh['gx_0'=4,'gx_1'=2,'gy_0'=4,'gy_1'=4] {'gx_0'}, use_global_device_ids=true, to_apply=%region_41.0 | all-reduce | flops 1 | bytes 8 | tf_op jit(solution)/shard_map/psum | solution.py:28
  455.8 10.0 %psum.314 = f32[]{:T(128)} all-reduce(f32[]{:T(128)} %psum.313), channel_id=1, replica_groups=mesh['gx_0'=4,'gx_1'=2,'gy_0'=4,'gy_1'=4] {'gy_0'}, use_global_device_ids=true, to_apply=%region_43.0 | all-reduce | flops 1 | bytes 8 | tf_op jit(solution)/shard_map/psum | solution.py:28
  495.4 325.5 %while.13 = (s32[]{:T(128)}, f32[8,128,128]{2,1,0:T(8,128)}, f32[8,2,128]{2,1,0:T(2,128)S(1)}, f32[128,112]{0,1:T(8,128)S(1)}, f32[8,128,128]{2,1,0:T(8,128)S(1)}, /*index=5*/f32[112]{0:T(128)S(1)}, s32[]{:T(128)}) while((s32[]{:T(128)}, f32[8,128,128]{2,1,0:T(8,128)}, f32[8,2,128]{2,1,0:T(2,128)S(1)}, ...), condition=%wide.region_56.57_spmd.clone, body=%wide.region_55.56_spmd.clone.sunk | while | flops 2860824576 | bytes 88995904 | solution.py:179
  498.0 15.5 %fusion.207 = f32[14336,128]{1,0:T(8,128)} fusion(f32[16,8,112,128]{3,2,1,0:T(8,128)S(1)} %bitcast.114), kind=kOutput, calls=%fused_computation.6.clone.1 | convolution fusion | flops 2818605056 | bytes 14680064 | tf_op jit(solution)/shard_map/while/body/eval_jaxpr/dot_general | solution.py:97
  538.6 15.5 %fusion.207 = f32[14336,128]{1,0:T(8,128)} fusion(f32[16,8,112,128]{3,2,1,0:T(8,128)S(1)} %bitcast.114), kind=kOutput, calls=%fused_computation.6.clone.1 | convolution fusion | flops 2818605056 | bytes 14680064 | tf_op jit(solution)/shard_map/while/body/eval_jaxpr/dot_general | solution.py:97
  579.2 15.5 %fusion.207 = f32[14336,128]{1,0:T(8,128)} fusion(f32[16,8,112,128]{3,2,1,0:T(8,128)S(1)} %bitcast.114), kind=kOutput, calls=%fused_computation.6.clone.1 | convolution fusion | flops 2818605056 | bytes 14680064 | tf_op jit(solution)/shard_map/while/body/eval_jaxpr/dot_general | solution.py:97
  619.8 15.5 %fusion.207 = f32[14336,128]{1,0:T(8,128)} fusion(f32[16,8,112,128]{3,2,1,0:T(8,128)S(1)} %bitcast.114), kind=kOutput, calls=%fused_computation.6.clone.1 | convolution fusion | flops 2818605056 | bytes 14680064 | tf_op jit(solution)/shard_map/while/body/eval_jaxpr/dot_general | solution.py:97
  660.4 15.5 %fusion.207 = f32[14336,128]{1,0:T(8,128)} fusion(f32[16,8,112,128]{3,2,1,0:T(8,128)S(1)} %bitcast.114), kind=kOutput, calls=%fused_computation.6.clone.1 | convolution fusion | flops 2818605056 | bytes 14680064 | tf_op jit(solution)/shard_map/while/body/eval_jaxpr/dot_general | solution.py:97
  701.0 15.5 %fusion.207 = f32[14336,128]{1,0:T(8,128)} fusion(f32[16,8,112,128]{3,2,1,0:T(8,128)S(1)} %bitcast.114), kind=kOutput, calls=%fused_computation.6.clone.1 | convolution fusion | flops 2818605056 | bytes 14680064 | tf_op jit(solution)/shard_map/while/body/eval_jaxpr/dot_general | solution.py:97
  741.7 15.5 %fusion.207 = f32[14336,128]{1,0:T(8,128)} fusion(f32[16,8,112,128]{3,2,1,0:T(8,128)S(1)} %bitcast.114), kind=kOutput, calls=%fused_computation.6.clone.1 | convolution fusion | flops 2818605056 | bytes 14680064 | tf_op jit(solution)/shard_map/while/body/eval_jaxpr/dot_general | solution.py:97
  782.3 15.5 %fusion.207 = f32[14336,128]{1,0:T(8,128)} fusion(f32[16,8,112,128]{3,2,1,0:T(8,128)S(1)} %bitcast.114), kind=kOutput, calls=%fused_computation.6.clone.1 | convolution fusion | flops 2818605056 | bytes 14680064 | tf_op jit(solution)/shard_map/while/body/eval_jaxpr/dot_general | solution.py:97
  859.7 9.2 %psum.318 = f32[]{:T(128)} all-reduce(f32[]{:T(128)} %psum.317), channel_id=1, replica_groups=mesh['gx_0'=4,'gx_1'=2,'gy_0'=4,'gy_1'=4] {'gy_0'}, use_global_device_ids=true, to_apply=%region_48.0 | all-reduce | flops 1 | bytes 8 | tf_op jit(solution)/shard_map/psum | solution.py:28
  868.8 10.7 %psum.319 = f32[]{:T(128)} all-reduce(f32[]{:T(128)} %psum.318), channel_id=1, replica_groups=mesh['gx_0'=4,'gx_1'=2,'gy_0'=4,'gy_1'=4] {'gy_1'}, use_global_device_ids=true, to_apply=%region_49.0 | all-reduce | flops 1 | bytes 8 | tf_op jit(solution)/shard_map/psum | solution.py:28
  (387 shorter events, 509.6 us)
Async XLA Ops:
  2.3 69.5 %collective-permute-start.7 = (f32[1,128,128]{1,0,2:T(1,128)}, f32[1,128,128]{1,0,2:T(1,128)S(1)}, u32[]{:S(2)}, u32[]{:S(2)}) collective-permute-start(f32[1,128,128]{1,0,2:T(1,128)} %copy.162), channel_id=1, source_target_pairs={{0,1},{1,2},{2,3},{3,4},{4,5},{5,6},{6,7},{7,8},{8,9},{9,10},{10,1... | collective-permute-start | bytes 196616 | tf_op jit(solution)/shard_map/ppermute | solution.py:20
  6.5 65.3 %collective-permute-start.5 = (f32[1,128,128]{1,0,2:T(1,128)}, f32[1,128,128]{1,0,2:T(1,128)}, u32[]{:S(2)}, u32[]{:S(2)}) collective-permute-start(f32[1,128,128]{1,0,2:T(1,128)} %copy.156), channel_id=1, source_target_pairs={{1,0},{2,1},{3,2},{4,3},{5,4},{6,5},{7,6},{8,7},{9,8},{10,9},{11,1... | collective-permute-start | bytes 196616 | tf_op jit(solution)/shard_map/ppermute | solution.py:21
  13.3 50.5 %collective-permute-start.3 = (f32[16,128,1]{1,0,2:T(8,128)}, f32[16,128,1]{1,0,2:T(8,128)S(1)}, u32[]{:S(2)}, u32[]{:S(2)}) collective-permute-start(f32[16,128,1]{1,0,2:T(8,128)} %get-tuple-element.154), channel_id=1, source_target_pairs={{0,16},{16,32},{32,48},{48,64},{64,80},{80,96},{96,112},{112,0},{1... | collective-permute-start | bytes 24584 | tf_op jit(solution)/shard_map/ppermute | solution.py:20
  13.3 50.7 %collective-permute-start.1 = (f32[16,128,1]{1,0,2:T(8,128)S(1)}, f32[16,128,1]{1,0,2:T(8,128)S(1)}, u32[]{:S(2)}, u32[]{:S(2)}) collective-permute-start(f32[16,128,1]{1,0,2:T(8,128)S(1)} %get-tuple-element.153), channel_id=1, source_target_pairs={{16,0},{32,16},{48,32},{64,48},{80,64},{96,80},{112,96},{0,112},{1... | collective-permute-start | bytes 24584 | tf_op jit(solution)/shard_map/ppermute | solution.py:21
  16.8 385.0 %copy-start.1 = (f32[16,128,128]{1,0,2:T(8,128)}, f32[16,128,128]{1,0,2:T(8,128)S(1)}, u32[]{:S(2)}) copy-start(f32[16,128,128]{1,0,2:T(8,128)S(1)} %copy.142) | copy-start | bytes 3145732
  16.8 51.2 %collective-permute-start = (f32[16,128,1]{1,0,2:T(8,128)S(1)}, f32[16,128,1]{1,0,2:T(8,128)S(1)}, u32[]{:S(2)}, u32[]{:S(2)}) collective-permute-start(f32[16,128,1]{1,0,2:T(8,128)S(1)} %get-tuple-element.152), channel_id=1, source_target_pairs={{16,0},{32,16},{48,32},{64,48},{80,64},{96,80},{112,96},{0,112},{1... | collective-permute-start | bytes 24584 | tf_op jit(solution)/shard_map/ppermute | solution.py:21
  63.8 7.9 collective-permute-start.2
  64.0 7.8 collective-permute-start.4
  68.0 333.8 %copy-start.17 = (f32[16,128,1]{1,0,2:T(8,128)}, f32[16,128,1]{1,0,2:T(8,128)S(1)}, u32[]{:S(2)}) copy-start(f32[16,128,1]{1,0,2:T(8,128)S(1)} %collective-permute-done) | copy-start | bytes 24580
  68.1 8.3 collective-permute-start.6
  83.0 11.2 %collective-permute-start.11 = (f32[1,128,128]{1,0,2:T(1,128)S(1)}, f32[1,128,128]{1,0,2:T(1,128)S(1)}, u32[]{:S(2)}, u32[]{:S(2)}) collective-permute-start(f32[1,128,128]{1,0,2:T(1,128)S(1)} %get-tuple-element.148), channel_id=1, source_target_pairs={{0,1},{1,2},{2,3},{3,4},{4,5},{5,6},{6,7},{7,8},{8,9},{9,10},{10,1... | collective-permute-start | bytes 196616 | tf_op jit(solution)/shard_map/ppermute | solution.py:20
  84.9 9.3 %collective-permute-start.10 = (f32[1,128,128]{1,0,2:T(1,128)S(1)}, f32[1,128,128]{1,0,2:T(1,128)S(1)}, u32[]{:S(2)}, u32[]{:S(2)}) collective-permute-start(f32[1,128,128]{1,0,2:T(1,128)S(1)} %get-tuple-element.147), channel_id=1, source_target_pairs={{1,0},{2,1},{3,2},{4,3},{5,4},{6,5},{7,6},{8,7},{9,8},{10,9},{11,1... | collective-permute-start | bytes 196616 | tf_op jit(solution)/shard_map/ppermute | solution.py:21
  91.0 3.1 collective-permute-start.9
  91.0 3.2 collective-permute-start.8
  170.2 11.5 %collective-permute-start.15 = (f32[1,128,128]{1,0,2:T(1,128)S(1)}, f32[1,128,128]{1,0,2:T(1,128)S(1)}, u32[]{:S(2)}, u32[]{:S(2)}) collective-permute-start(f32[1,128,128]{1,0,2:T(1,128)S(1)} %get-tuple-element.144), channel_id=1, source_target_pairs={{0,1},{1,2},{2,3},{3,4},{4,5},{5,6},{6,7},{7,8},{8,9},{9,10},{10,1... | collective-permute-start | bytes 196616 | tf_op jit(solution)/shard_map/ppermute | solution.py:20
  173.7 8.1 collective-permute-start.14
  178.3 3.3 collective-permute-start.13
  178.4 3.3 collective-permute-start.12
  249.1 240.7 %all-to-all-start = ((f32[128,130,16]{1,2,0:T(8,128)}), f32[128,130,16]{1,2,0:T(8,128)}, u32[]{:S(2)}, u32[]{:S(2)}) async-start(f32[128,130,16]{1,2,0:T(8,128)} %multiply_bitcast_fusion), calls=%async_computation | async-start | bytes 4194304 | tf_op jit(solution)/shard_map/all_to_all | solution.py:166
  299.6 11.3 %collective-permute-start.19 = (f32[1,128,128]{1,0,2:T(1,128)S(1)}, f32[1,128,128]{1,0,2:T(1,128)S(1)}, u32[]{:S(2)}, u32[]{:S(2)}) collective-permute-start(f32[1,128,128]{1,0,2:T(1,128)S(1)} %get-tuple-element.140), channel_id=1, source_target_pairs={{0,1},{1,2},{2,3},{3,4},{4,5},{5,6},{6,7},{7,8},{8,9},{9,10},{10,1... | collective-permute-start | bytes 196616 | tf_op jit(solution)/shard_map/ppermute | solution.py:20
  301.5 9.4 %collective-permute-start.18 = (f32[1,128,128]{1,0,2:T(1,128)S(1)}, f32[1,128,128]{1,0,2:T(1,128)S(1)}, u32[]{:S(2)}, u32[]{:S(2)}) collective-permute-start(f32[1,128,128]{1,0,2:T(1,128)S(1)} %get-tuple-element.139), channel_id=1, source_target_pairs={{1,0},{2,1},{3,2},{4,3},{5,4},{6,5},{7,6},{8,7},{9,8},{10,9},{11,1... | collective-permute-start | bytes 196616 | tf_op jit(solution)/shard_map/ppermute | solution.py:21
  307.5 3.3 collective-permute-start.17
  307.6 3.3 collective-permute-start.16
  390.5 11.3 %collective-permute-start.23 = (f32[1,128,128]{1,0,2:T(1,128)S(1)}, f32[1,128,128]{1,0,2:T(1,128)S(1)}, u32[]{:S(2)}, u32[]{:S(2)}) collective-permute-start(f32[1,128,128]{1,0,2:T(1,128)S(1)} %get-tuple-element.136), channel_id=1, source_target_pairs={{0,1},{1,2},{2,3},{3,4},{4,5},{5,6},{6,7},{7,8},{8,9},{9,10},{10,1... | collective-permute-start | bytes 196616 | tf_op jit(solution)/shard_map/ppermute | solution.py:20
  394.4 7.4 collective-permute-start.22
  398.5 3.3 collective-permute-start.21
  398.5 3.3 collective-permute-start.20
  478.2 362.1 %collective-permute-start.27 = (f32[1,128,128]{1,0,2:T(1,128)}, f32[1,128,128]{1,0,2:T(1,128)}, u32[]{:S(2)}, u32[]{:S(2)}) collective-permute-start(f32[1,128,128]{1,0,2:T(1,128)} %get-tuple-element.132), channel_id=1, source_target_pairs={{0,1},{1,2},{2,3},{3,4},{4,5},{5,6},{6,7},{7,8},{8,9},{9,10},{10,1... | collective-permute-start | bytes 196616 | tf_op jit(solution)/shard_map/ppermute | solution.py:20
  482.1 358.2 %collective-permute-start.26 = (f32[1,128,128]{1,0,2:T(1,128)}, f32[1,128,128]{1,0,2:T(1,128)}, u32[]{:S(2)}, u32[]{:S(2)}) collective-permute-start(f32[1,128,128]{1,0,2:T(1,128)} %get-tuple-element.131), channel_id=1, source_target_pairs={{1,0},{2,1},{3,2},{4,3},{5,4},{6,5},{7,6},{8,7},{9,8},{10,9},{11,1... | collective-permute-start | bytes 196616 | tf_op jit(solution)/shard_map/ppermute | solution.py:21
  486.8 353.5 %collective-permute-start.25 = (f32[16,128,1]{1,0,2:T(8,128)}, f32[16,128,1]{1,0,2:T(8,128)}, u32[]{:S(2)}, u32[]{:S(2)}) collective-permute-start(f32[16,128,1]{1,0,2:T(8,128)} %get-tuple-element.130), channel_id=1, source_target_pairs={{0,16},{16,32},{32,48},{48,64},{64,80},{80,96},{96,112},{112,0},{1... | collective-permute-start | bytes 24584 | tf_op jit(solution)/shard_map/ppermute | solution.py:20
  486.8 353.5 %collective-permute-start.24 = (f32[16,128,1]{1,0,2:T(8,128)}, f32[16,128,1]{1,0,2:T(8,128)}, u32[]{:S(2)}, u32[]{:S(2)}) collective-permute-start(f32[16,128,1]{1,0,2:T(8,128)} %get-tuple-element.129), channel_id=1, source_target_pairs={{16,0},{32,16},{48,32},{64,48},{80,64},{96,80},{112,96},{0,112},{1... | collective-permute-start | bytes 24584 | tf_op jit(solution)/shard_map/ppermute | solution.py:21
  832.5 57.0 %all-to-all-start.1 = ((f32[128,128,16]{1,2,0:T(8,128)}), f32[128,128,16]{1,2,0:T(8,128)S(1)}, u32[]{:S(2)}, u32[]{:S(2)}) async-start(f32[128,128,16]{1,2,0:T(8,128)} %multiply_bitcast_fusion.2), calls=%async_computation.1 | async-start | bytes 2097152 | tf_op jit(solution)/shard_map/all_to_all | solution.py:187
  (50 other events, 2988.0 us)
where the time goes:
time: 914 us; the launch traced here: 897 us
  blocking collectives  331 us (36%)
  local copies, waits for them, and re-layouts  182 us (20%)
  matrix products  175 us (19%)
  other arithmetic  105 us (11%)
  starting transfers between devices  81.7 us (9%)
  between operations  15.5 us (2%)
    psum x36, blocking collectives, one_axis_at_a_time(): array = lax.psum(array, axis)  300 us
    dot_general x8, matrix products, radiate(): jnp.dot(triangle, thickness.reshape(levels, gpoints * columns), precision...  124 us
    reshape x8, local copies, waits for them, and re-layouts, radiate(): cumulative = cumulative.reshape(levels, gpoints, columns)  67.7 us
    dot_general x8, matrix products, radiate(): jnp.einsum('lgc,g->lc', downward - upward, solar_weight, precision=lax.Pr...  51.3 us
    slice x8, local copies, waits for them, and re-layouts, radiate(): cumulative[-1] - cumulative  49.3 us
    ppermute x14, starting transfers between devices, padded(): after = lax.ppermute(first, axis, down)  43.7 us
    reduce_sum x5, other arithmetic, body(): curvature_sum = one_axis_at_a_time(jnp.sum(direction * applied), GX_GY)  24.8 us
    all_gather x3, blocking collectives, stacked_from(): blocks = lax.all_gather(blocks, axes[k])  23.8 us
  transfers between devices with their start and end apart: 30, of which 3 were waited for; matrix products, arithmetic and copies ran while one was open for 46% of the time, Pallas kernels for 0%

commit v1 on v0

v1 whole, which is shorter than its diff:
```python
import functools
import math

import jax
import jax.numpy as jnp
from jax import lax
from jax.experimental import pallas as pl
from jax.experimental.pallas import tpu as pltpu
from jax.sharding import PartitionSpec as P

ITERS = 5
DEPTH = ITERS + 1
SLOT = 8
PAD = 8
CHUNK = 32
CENTRE = 14.0
HALF = 13.0
TRUST = 500.0
LOG2E = math.log2(math.e)
GX, GY = ("gx", "gy")
F32 = jnp.float32


def ring(axis, step):
    n = lax.axis_size(axis)
    return [(i, (i + step) % n) for i in range(n)]


def line(axis, step):
    n = lax.axis_size(axis)
    return [(i, i + step) for i in range(n) if 0 <= i + step < n]


def lanes(shape):
    return lax.broadcasted_iota(jnp.int32, shape, len(shape) - 1)


def edges_kernel(state, diff, north, south, east, west):
    rows, levels, width = state.shape
    for f, source in enumerate((state, diff)):
        south[f * DEPTH : (f + 1) * DEPTH] = source[:DEPTH]
        north[f * DEPTH : (f + 1) * DEPTH] = source[rows - DEPTH :]

        @pl.loop(0, levels // CHUNK)
        def _(c):
            at = pl.ds(pl.multiple_of(c * CHUNK, CHUNK), CHUNK)
            lane = lanes((CHUNK, width))
            to_west = jnp.zeros((CHUNK, width), F32)
            to_east = jnp.zeros((CHUNK, width), F32)
            for r in range(rows):
                x = source[r, at, :]
                mine = (lane >= r * SLOT) & (lane < (r + 1) * SLOT)
                w = pltpu.roll(x, r * SLOT, 1) if r else x
                to_west = jnp.where(mine, w, to_west)
                e = pltpu.roll(x, (r * SLOT + DEPTH) % width, 1)
                to_east = jnp.where(mine, e, to_east)
            west[f, at, :] = to_west
            east[f, at, :] = to_east


def edges(state, diff):
    rows, levels, width = state.shape
    tall = jax.ShapeDtypeStruct((2 * DEPTH, levels, width), F32)
    thin = jax.ShapeDtypeStruct((2, levels, width), F32)
    return pl.pallas_call(
        edges_kernel,
        out_shape=(tall, tall, thin, thin),
        compiler_params=pltpu.CompilerParams(vmem_limit_bytes=24 << 20),
        cost_estimate=pl.CostEstimate(
            flops=1 << 20, bytes_accessed=4 << 20, transcendentals=0
        ),
        name="edges",
    )(state, diff)


def basis_kernel(
    state, diff, north, south, east, west, north_side, south_side, vectors, moments, *work
):
    ce, cn, cl, cu, va, vb, vc = work
    rows, levels, width = state.shape
    total = rows + 2 * DEPTH
    ring_buffers = (va, vb, vc)
    for buffer in ring_buffers:

        @pl.loop(0, total)
        def _(r):
            for t in range(2):
                buffer[r, t, :PAD, :] = jnp.zeros((PAD, width), F32)
                buffer[r, t, PAD + levels :, :] = jnp.zeros((PAD, width), F32)

    @pl.loop(0, levels // CHUNK)
    def _(c):
        at = pl.ds(pl.multiple_of(c * CHUNK, CHUNK), CHUNK)
        to = pl.ds(pl.multiple_of(c * CHUNK + PAD, PAD), CHUNK)
        lane = lanes((CHUNK, width))
        for f, (own, target) in enumerate(((state, va), (diff, vb))):
            for r in range(total):
                if r < DEPTH:
                    x = south[f * DEPTH + r, at, :]
                    e, w = south_side[f, at, :], south_side[2 + f, at, :]
                    slot = rows - DEPTH + r
                elif r < DEPTH + rows:
                    x = own[r - DEPTH, at, :]
                    e, w = east[f, at, :], west[f, at, :]
                    slot = r - DEPTH
                else:
                    slot = r - DEPTH - rows
                    x = north[f * DEPTH + slot, at, :]
                    e, w = north_side[f, at, :], north_side[2 + f, at, :]
                up = (width - slot * SLOT) % width
                e = pltpu.roll(e, up, 1) if up else e
                down = (2 * width - DEPTH - slot * SLOT) % width
                w = pltpu.roll(w, down, 1) if down else w
                side = jnp.where(lane < DEPTH, e, jnp.where(lane >= width - DEPTH, w, 0.0))
                if f:
                    x, side = jnp.sqrt(x), jnp.sqrt(side)
                target[r, 0, to, :] = x
                target[r, 1, to, :] = side

    def eastward(v0, v1):
        last = lanes(v0.shape) == width - 1
        a, b = pltpu.roll(v0, width - 1, 1), pltpu.roll(v1, width - 1, 1)
        return jnp.where(last, b, a), jnp.where(last, a, b)

    def westward(v0, v1):
        first = lanes(v0.shape) == 0
        a, b = pltpu.roll(v0, 1, 1), pltpu.roll(v1, 1, 1)
        return jnp.where(first, b, a), jnp.where(first, a, b)

    @pl.loop(0, total)
    def _(r):
        beyond = jnp.minimum(r + 1, total - 1)
        for c in range(levels // CHUNK):
            lo = PAD + c * CHUNK
            q = [vb[r, t, lo : lo + CHUNK, :] for t in range(2)]
            nearby = eastward(*q)
            for t in range(2):
                at = slice(c * CHUNK, (c + 1) * CHUNK)
                ce[r, t, at, :] = q[t] * nearby[t]
                cn[r, t, at, :] = q[t] * vb[beyond, t, lo : lo + CHUNK, :]
                cl[r, t, at, :] = q[t] * vb[r, t, lo + 1 : lo + CHUNK + 1, :]
                cu[r, t, at, :] = q[t] * vb[r, t, lo - 1 : lo + CHUNK - 1, :]

    def apply(k, source, older, target):
        def row(r, sums):
            own = sums is not None
            for c in range(levels // CHUNK):
                lo = PAD + c * CHUNK
                at = slice(c * CHUNK, (c + 1) * CHUNK)
                v = [source[r, t, lo : lo + CHUNK, :] for t in range(2)]
                nearby = eastward(*v)
                east_flux = [ce[r, t, at, :] * (v[t] - nearby[t]) for t in range(2)]
                west_flux = westward(*east_flux)
                for t in range(2):
                    spread = east_flux[t] - west_flux[t]
                    spread += cn[r, t, at, :] * (v[t] - source[r + 1, t, lo : lo + CHUNK, :])
                    spread += cn[r - 1, t, at, :] * (v[t] - source[r - 1, t, lo : lo + CHUNK, :])
                    spread += cl[r, t, at, :] * (v[t] - source[r, t, lo + 1 : lo + CHUNK + 1, :])
                    spread += cu[r, t, at, :] * (v[t] - source[r, t, lo - 1 : lo + CHUNK - 1, :])
                    if k == 0:
                        new = -spread
                    elif k == 1:
                        new = (spread + (1.0 - CENTRE) * v[t]) * (1.0 / HALF)
                    else:
                        new = (spread + (1.0 - CENTRE) * v[t]) * (2.0 / HALF)
                        new = new - older[r, t, lo : lo + CHUNK, :]
                    if k < ITERS:
                        target[r, t, lo : lo + CHUNK, :] = new
                    if own and t == 0:
                        vectors[k, r - DEPTH, at, :] = new
                        both = [new * new] if k < ITERS else []
                        if k:
                            both.append(new * v[0])
                        folded = [p.reshape(CHUNK // 8, 8, width).sum(0) for p in both]
                        sums = tuple(s + p for s, p in zip(sums, folded))
            return sums

        def halo(r):
            row(r, None)

        if k + 1 < DEPTH:
            pl.loop(k + 1, DEPTH)(halo)
            pl.loop(DEPTH + rows, total - 1 - k)(halo)
        count = 1 if k in (0, ITERS) else 2
        zero = jnp.zeros((8, width), F32)
        sums = lax.fori_loop(DEPTH, DEPTH + rows, row, (zero,) * count)
        first = [2 * k, 2 * k - 1] if k < ITERS else [2 * k - 1]
        for place, part in zip(first, sums):
            moments[place : place + 1, :] = jnp.sum(part, 0, keepdims=True)

    moments[...] = jnp.zeros_like(moments)
    apply(0, va, None, vb)
    order = (vb, vc, va)
    for k in range(1, DEPTH):
        apply(k, order[(k - 1) % 3], order[(k - 2) % 3], order[k % 3])


def basis(*arrays):
    rows, levels, width = arrays[0].shape
    total = rows + 2 * DEPTH
    return pl.pallas_call(
        basis_kernel,
        out_shape=(
            jax.ShapeDtypeStruct((DEPTH, rows, levels, width), F32),
            jax.ShapeDtypeStruct((16, width), F32),
        ),
        scratch_shapes=[pltpu.VMEM((total, 2, levels, width), F32)] * 4
        + [pltpu.VMEM((total, 2, levels + 2 * PAD, width), F32)] * 3,
        compiler_params=pltpu.CompilerParams(vmem_limit_bytes=48 << 20),
        cost_estimate=pl.CostEstimate(
            flops=100 << 20, bytes_accessed=14 << 20, transcendentals=0
        ),
        name="basis",
    )(*arrays)


def coefficients(sums):
    zero = jnp.zeros_like(sums[0])
    one = zero + 1.0
    mom = []
    for k in range(ITERS):
        mom.append(2.0 * sums[2 * k] - (mom[0] if k else sums[0]))
        mom.append(2.0 * sums[2 * k + 1] - (mom[1] if k else sums[1]))

    gram = {}
    for j in range(DEPTH):
        for k in range(j, DEPTH):
            if j + k < 2 * ITERS:
                gram[j, k] = gram[k, j] = 0.5 * (mom[j + k] + mom[k - j])

    def inner(a, b):
        value = size = zero
        for j, p in enumerate(a):
            for k, q in enumerate(b):
                term = p * q * gram[j, k]
                value, size = value + term, size + jnp.abs(term)
        return value, size

    def image(p):
        out = [CENTRE * q for q in p] + [zero]
        for k, q in enumerate(p):
            if k == 0:
                out[1] = out[1] + HALF * q
            else:
                out[k - 1] = out[k - 1] + 0.5 * HALF * q
                out[k + 1] = out[k + 1] + 0.5 * HALF * q
        return out

    def combined(a, scale, b):
        n = max(len(a), len(b))
        a, b = [list(x) + [zero] * (n - len(x)) for x in (a, b)]
        return [p + scale * q for p, q in zip(a, b)]

    residual, direction, field = [one], [one], []
    current, loss = mom[0], one
    for k in range(ITERS):
        applied = image(direction)
        curvature, size = inner(direction, applied)
        loss = jnp.maximum(loss, jnp.where(size < TRUST * curvature, one, 2.0 * one))
        step = current / curvature
        field = combined(field, step, direction)
        residual = combined(residual, -step, applied)
        if k < ITERS - 1:
            following, size = inner(residual, residual)
            loss = jnp.maximum(loss, jnp.where(size < TRUST * following, one, 2.0 * one))
            direction = combined(residual, following / current, direction)
            current = following
    return field, residual, loss


def recombine_kernel(moments, state, vectors, new_state, residual, loss, weights):
    @pl.when(pl.program_id(0) == 0)
    def _():
        width = moments.shape[1]
        sums = [
            jnp.broadcast_to(jnp.sum(moments[i : i + 1, :], 1, keepdims=True), (8, width))
            for i in range(2 * ITERS)
        ]
        field, rest, bad = coefficients(sums)
        for i, value in enumerate(field + rest):
            weights[i] = value
        loss[...] = bad

    levels, width = state.shape[1:]

    def weighted(i, x):
        return (x.reshape(levels // 8, 8, width) * weights[i]).reshape(levels, width)

    x, r = state[0], None
    for k in range(DEPTH):
        v = vectors[k, 0]
        if k < ITERS:
            x = x + weighted(k, v)
        part = weighted(ITERS + k, v)
        r = part if r is None else r + part
    new_state[0] = x
    residual[0] = r


def recombine(moments, state, vectors):
    rows, levels, width = state.shape
    block = pl.BlockSpec((1, levels, width), lambda j: (j, 0, 0))
    stack = pl.BlockSpec((DEPTH, 1, levels, width), lambda j: (0, j, 0, 0))
    whole = lambda *s: pl.BlockSpec(s, lambda j: (0,) * len(s))
    like = jax.ShapeDtypeStruct(state.shape, F32)
    return pl.pallas_call(
        recombine_kernel,
        grid=(rows,),
        out_shape=(like, like, jax.ShapeDtypeStruct((8, width), F32)),
        in_specs=[whole(16, width), block, stack],
        out_specs=(block, block, whole(8, width)),
        scratch_shapes=[pltpu.VMEM((ITERS + DEPTH, 8, width), F32)],
        compiler_params=pltpu.CompilerParams(vmem_limit_bytes=24 << 20),
        cost_estimate=pl.CostEstimate(
            flops=6 << 20, bytes_accessed=9 << 20, transcendentals=0
        ),
        name="recombine",
    )(moments, state, vectors)


def flux_kernel(first, mask, state, vapour, cosine, albedo, across, spread, weight, *rest):
    out, slanted, upright = rest[-3:]
    j = first + pl.program_id(0)
    levels = state.shape[1]
    tiles = across.shape[0] // 8

    @pl.when(mask[j] == 0)
    def _():
        out[...] = jnp.zeros_like(out)

    @pl.when(mask[j] != 0)
    def _():
        optical = vapour[0] * (1.0 + 0.5 * jnp.tanh(state[0]))
        mu = cosine[0]
        slant = LOG2E / mu
        slanted[...] = optical * -slant
        upright[...] = optical * (1.66 * LOG2E)
        total = jnp.dot(
            across[...], optical, precision=lax.Precision.HIGHEST, preferred_element_type=F32
        )
        down = jnp.log2(weight[...] * mu)
        up = down + jnp.log2(albedo[0]) - total * (slant + 1.66 * LOG2E)
        sub = lax.broadcasted_iota(jnp.int32, (8, 128), 0)
        cut = lambda x: tuple(x[8 * t : 8 * t + 8] for t in range(tiles))

        def eight_levels(i, carry):
            down, up = (list(c) for c in carry)
            result = jnp.zeros((8, 128), F32)
            for k in range(8):
                level = i * 8 + k
                o1 = jnp.broadcast_to(slanted[pl.ds(level, 1), :], (8, 128))
                o2 = jnp.broadcast_to(upright[pl.ds(level, 1), :], (8, 128))
                net = None
                for t in range(tiles):
                    a = spread[level, 8 * t : 8 * t + 8, :]
                    down[t] = down[t] + a * o1
                    up[t] = up[t] + a * o2
                    one = jnp.exp2(down[t]) - jnp.exp2(up[t])
                    net = one if net is None else net + one
                result = jnp.where(sub == k, jnp.sum(net, 0, keepdims=True), result)
            out[0, pl.ds(pl.multiple_of(i * 8, 8), 8), :] = result
            return tuple(down), tuple(up)

        lax.fori_loop(0, levels // 8, eight_levels, (cut(down), cut(up)))


def fluxes(first, count, mask, fields, tables, before):
    state = fields[0]
    rows, levels, width = state.shape
    g = tables[0].shape[0]
    block = pl.BlockSpec((1, levels, width), lambda j, m: (first + j, 0, 0))
    row = pl.BlockSpec((1, 1, width), lambda j, m: (first + j, 0, 0))
    whole = lambda *s: pl.BlockSpec(s, lambda j, m: (0,) * len(s))
    resident = pl.BlockSpec(memory_space=pltpu.VMEM)
    in_specs = [block, block, row, row, whole(g, levels), resident, whole(g, width)]
    held = () if before is None else (before,)
    if held:
        in_specs.append(pl.BlockSpec(memory_space=pl.ANY))
    return pl.pallas_call(
        functools.partial(flux_kernel, first),
        out_shape=jax.ShapeDtypeStruct(state.shape, F32),
        grid_spec=pltpu.PrefetchScalarGridSpec(
            num_scalar_prefetch=1,
            grid=(count,),
            in_specs=in_specs,
            out_specs=block,
            scratch_shapes=[pltpu.VMEM((levels, width), F32)] * 2,
        ),
        input_output_aliases={8: 0} if held else {},
        compiler_params=pltpu.CompilerParams(vmem_limit_bytes=20 << 20),
        cost_estimate=pl.CostEstimate(
            flops=count * (24 << 20), bytes_accessed=count * (6 << 20), transcendentals=count * (4 << 20)
        ),
        name="fluxes",
    )(mask, *fields, *tables, *held)


def shifted(values):
    width = values.shape[2]
    west = lax.ppermute(values[:, :, width - 1 :], GX, ring(GX, 1))
    east = lax.ppermute(values[:, :, :1], GX, ring(GX, -1))
    south = lax.ppermute(values[-1:], GY, line(GY, 1))
    north = lax.ppermute(values[:1], GY, line(GY, -1))
    wide = jnp.concatenate([west, values, east], 2)
    tall = jnp.concatenate([south, values, north], 0)
    return wide, tall


def plain(state, diff):
    wide, tall = shifted(diff)
    faces = [diff * wide[:, :, 2:], diff * wide[:, :, :-2], diff * tall[2:], diff * tall[:-2]]
    east, west, north, south = [jnp.sqrt(f) for f in faces]
    level = jnp.sqrt(diff[:, 1:] * diff[:, :-1])

    def operate(v):
        wide, tall = shifted(v)
        out = v + east * (v - wide[:, :, 2:]) + west * (v - wide[:, :, :-2])
        out = out + north * (v - tall[2:]) + south * (v - tall[:-2])
        flux = level * (v[:, 1:] - v[:, :-1])
        return out - jnp.pad(flux, ((0, 0), (0, 1), (0, 0))) + jnp.pad(flux, ((0, 0), (1, 0), (0, 0)))

    total = lambda a, b: lax.psum(lax.psum(jnp.sum(a * b), GX), GY)
    residual = state - operate(state)

    def iteration(_, carry):
        field, residual, direction, current = carry
        applied = operate(direction)
        step = current / total(direction, applied)
        field = field + step * direction
        residual = residual - step * applied
        following = total(residual, residual)
        return field, residual, residual + following / current * direction, following

    start = (state, residual, residual, total(residual, residual))
    return lax.fori_loop(0, ITERS, iteration, start)[:2]


def doubled(part, axis):
    n = lax.axis_size(axis)
    step = 1
    while step < n:
        other = lax.ppermute(part, axis, [(i, i ^ step) for i in range(n)])
        part = part + other
        step *= 2
    return part


def body(state, diff, vapour, cosine, albedo, absorption, weight, mask):
    rows, levels, width = state.shape
    g = absorption.shape[1]
    tables = (
        absorption.T,
        jnp.broadcast_to(absorption[:, :, None], (levels, g, width)),
        jnp.broadcast_to(weight[:, None], (g, width)),
    )
    fields = (state, vapour, cosine[:, None, :], albedo[:, None, :])

    to_north, to_south, to_east, to_west = edges(state, diff)
    east = lax.ppermute(to_west, GX, ring(GX, -1))
    west = lax.ppermute(to_east, GX, ring(GX, 1))
    south = lax.ppermute(to_north, GY, line(GY, 1))
    north = lax.ppermute(to_south, GY, line(GY, -1))
    sides = jnp.concatenate([east, west], 0)
    south_side = lax.ppermute(sides, GY, line(GY, 1))
    north_side = lax.ppermute(sides, GY, line(GY, -1))
    vectors, moments = basis(state, diff, north, south, east, west, north_side, south_side)
    moments = doubled(doubled(moments, GX), GY)
    new_state, residual, loss = recombine(moments, state, vectors)

    net = None
    first = 0
    for count in (6, 3) + (1,) * 7:
        net = fluxes(first, count, mask, fields, tables, net)
        first += count

    def untrusted(carry):
        return jnp.logical_not(carry[2] <= 1.0)

    def redo(carry):
        return (*plain(state, diff), jnp.ones((), F32))

    new_state, residual, _ = lax.while_loop(
        untrusted, redo, (new_state, residual, loss[0, 0])
    )
    return new_state, residual, net


def solution(mesh):
    block = P(GY, None, GX)
    in_specs = (block, block, block, P(GY, GX), P(GY, GX), P(), P(), P((GX, GY)))
    return jax.shard_map(
        body, mesh=mesh, in_specs=in_specs, out_specs=(block,) * 3, check_vma=False
    )
```

time: 914 us -> 163 us (0.18)
  the two profiles are of different devices: /device:TPU:100 before, /device:TPU:18 now
where the time goes in v1:
time: 163 us; the launch traced here: 162 us
  Pallas kernels  84 us (52%)
  starting transfers between devices  35.7 us (22%)
  local copies, waits for them, and re-layouts  22.2 us (14%)
  waiting for transfers between devices  18.1 us (11%)
    pallas_call x9, Pallas kernels, fluxes(): pl.pallas_call(functools.partial(flux_kernel, first), out_shape=jax.Shape...  46.4 us
    pallas_call x1, Pallas kernels, basis(): pl.pallas_call(basis_kernel, out_shape=(jax.ShapeDtypeStruct((DEPTH, rows...  34.1 us
    ppermute x7, starting transfers between devices, doubled(): other = lax.ppermute(part, axis, [(i, i ^ step) for i in range(n)])  19.7 us
    unnamed x36, local copies, waits for them, and re-layouts  14 us
    while x4, local copies, waits for them, and re-layouts, body(): lax.while_loop(untrusted, redo, (new_state, residual, loss[0, 0]))  5.52 us
    ppermute x7, waiting for transfers between devices, doubled(): other = lax.ppermute(part, axis, [(i, i ^ step) for i in range(n)])  5.25 us
    ppermute x1, waiting for transfers between devices, body(): north_side = lax.ppermute(sides, GY, line(GY, -1))  5.15 us
    ppermute x1, starting transfers between devices, body(): south_side = lax.ppermute(sides, GY, line(GY, 1))  4.86 us
  transfers between devices with their start and end apart: 13, of which 8 were waited for; matrix products, arithmetic and copies ran while one was open for 4% of the time, Pallas kernels for 29%

profile of v1, /device:TPU:18, one launch (start us, length us, event | category | flops | bytes accessed | tf_op | source)
XLA Modules:
  0.0 161.8 jit_solution(16802064207862175997)
XLA Ops:
  3.1 1.7 %edges.1 = (f32[12,128,128]{2,1,0:T(8,128)S(1)}, f32[12,128,128]{2,1,0:T(8,128)S(1)}, f32[2,128,128]{2,1,0:T(8,128)S(1)}, f32[2,128,128]{2,1,0:T(8,128)S(1)}) custom-call(f32[16,128,128]{2,1,0:T(8,128)S(1)} %copy-done.2, f32[16,128,128]{2,1,0:T(8,128)S(1)} %copy-done.6), custom_call_target="tpu_custom_call" | custom-call | flops 1048576 | bytes 4194304 | tf_op jit(solution)/shard_map/edges/pallas_call | solution.py:65
  4.8 2.4 %collective-permute-start.12 = (f32[12,128,128]{2,1,0:T(8,128)S(1)}, f32[12,128,128]{2,1,0:T(8,128)S(1)}, u32[]{:S(2)}, u32[]{:S(2)}) collective-permute-start(f32[12,128,128]{2,1,0:T(8,128)S(1)} %get-tuple-element.188), channel_id=1, source_target_pairs={{1,0},{2,1},{3,2},{4,3},{5,4},{6,5},{7,6},{8,7},{9,8},{10,9},{11,1... | collective-permute-start | bytes 2359304 | tf_op jit(solution)/shard_map/ppermute | solution.py:462
  7.2 3.5 %collective-permute-start.13 = (f32[12,128,128]{2,1,0:T(8,128)S(1)}, f32[12,128,128]{2,1,0:T(8,128)S(1)}, u32[]{:S(2)}, u32[]{:S(2)}) collective-permute-start(f32[12,128,128]{2,1,0:T(8,128)S(1)} %get-tuple-element.189), channel_id=1, source_target_pairs={{0,1},{1,2},{2,3},{3,4},{4,5},{5,6},{6,7},{7,8},{8,9},{9,10},{10,1... | collective-permute-start | bytes 2359304 | tf_op jit(solution)/shard_map/ppermute | solution.py:461
  10.7 2.9 %collective-permute-start.14 = (f32[2,128,128]{2,1,0:T(8,128)S(1)}, f32[2,128,128]{2,1,0:T(8,128)S(1)}, u32[]{:S(2)}, u32[]{:S(2)}) collective-permute-start(f32[2,128,128]{2,1,0:T(8,128)S(1)} %get-tuple-element.190), channel_id=1, source_target_pairs={{0,112},{16,0},{32,16},{48,32},{64,48},{80,64},{96,80},{112,96},{1... | collective-permute-start | bytes 393224 | tf_op jit(solution)/shard_map/ppermute | solution.py:459
  13.6 2.5 %collective-permute-done.14.east = f32[2,128,128]{2,1,0:T(8,128)S(1)} collective-permute-done((f32[2,128,128]{2,1,0:T(8,128)S(1)}, f32[2,128,128]{2,1,0:T(8,128)S(1)}, u32[]{:S(2)}, u32[]{:S(2)}) %collective-permute-start.14) | collective-permute-done | bytes 131104 | tf_op jit(solution)/shard_map/ppermute | solution.py:459
  16.1 3.1 %collective-permute-done.15.west = f32[2,128,128]{2,1,0:T(8,128)S(1)} collective-permute-done((f32[2,128,128]{2,1,0:T(8,128)S(1)}, f32[2,128,128]{2,1,0:T(8,128)S(1)}, u32[]{:S(2)}, u32[]{:S(2)}) %collective-permute-start.15) | collective-permute-done | bytes 131104 | tf_op jit(solution)/shard_map/ppermute | solution.py:460
  19.2 2.4 %collective-permute-start.16 = (f32[4,128,128]{2,1,0:T(8,128)S(1)}, f32[4,128,128]{2,1,0:T(8,128)S(1)}, u32[]{:S(2)}, u32[]{:S(2)}) collective-permute-start(f32[4,128,128]{2,1,0:T(8,128)S(1)} %constant_dynamic-update-slice_fusion), channel_id=1, source_target_pairs={{1,0},{2,1},{3,2},{4,3},{5,4},{6,5},{7,6},{8,7},{9,8},{10,9},{11,1... | collective-permute-start | bytes 786440 | tf_op jit(solution)/shard_map/ppermute | solution.py:465
  21.6 4.9 %collective-permute-start.17 = (f32[4,128,128]{2,1,0:T(8,128)S(1)}, f32[4,128,128]{2,1,0:T(8,128)S(1)}, u32[]{:S(2)}, u32[]{:S(2)}) collective-permute-start(f32[4,128,128]{2,1,0:T(8,128)S(1)} %constant_dynamic-update-slice_fusion), channel_id=1, source_target_pairs={{0,1},{1,2},{2,3},{3,4},{4,5},{5,6},{6,7},{7,8},{8,9},{9,10},{10,1... | collective-permute-start | bytes 786440 | tf_op jit(solution)/shard_map/ppermute | solution.py:464
  26.4 5.1 %collective-permute-done.16.north_side = f32[4,128,128]{2,1,0:T(8,128)S(1)} collective-permute-done((f32[4,128,128]{2,1,0:T(8,128)S(1)}, f32[4,128,128]{2,1,0:T(8,128)S(1)}, u32[]{:S(2)}, u32[]{:S(2)}) %collective-permute-start.16) | collective-permute-done | bytes 262176 | tf_op jit(solution)/shard_map/ppermute | solution.py:465
  31.6 2.1 %collective-permute-done.17.south_side = f32[4,128,128]{2,1,0:T(8,128)S(1)} collective-permute-done((f32[4,128,128]{2,1,0:T(8,128)S(1)}, f32[4,128,128]{2,1,0:T(8,128)S(1)}, u32[]{:S(2)}, u32[]{:S(2)}) %collective-permute-start.17) | collective-permute-done | bytes 262176 | tf_op jit(solution)/shard_map/ppermute | solution.py:464
  36.1 34.1 %basis.1 = (f32[6,16,128,128]{3,2,1,0:T(8,128)}, f32[16,128]{1,0:T(8,128)S(1)}) custom-call(f32[16,128,128]{2,1,0:T(8,128)S(1)} %copy-done.3, f32[16,128,128]{2,1,0:T(8,128)S(1)} %copy-done.7, f32[12,128,128]{2,1,0:T(8,128)S(1)} %collective-permute-done.12.north, f32[12,128,128]{2,1,0:T(8,128)S(1)} %collective-permute-done.13.south, ...), custom_call_target="tpu_custom_call" | custom-call | flops 104857600 | bytes 14680064 | tf_op jit(solution)/shard_map/basis/pallas_call | solution.py:201
  71.4 1.9 %collective-permute-start.19 = (f32[16,128]{1,0:T(8,128)S(1)}, f32[16,128]{1,0:T(8,128)S(1)}, u32[]{:S(2)}, u32[]{:S(2)}) collective-permute-start(f32[16,128]{1,0:T(8,128)S(1)} %add.113), channel_id=1, source_target_pairs={{0,32},{16,48},{32,0},{48,16},{64,96},{80,112},{96,64},{112,80},{1... | collective-permute-start | bytes 24584 | tf_op jit(solution)/shard_map/ppermute | solution.py:442
  73.3 1.7 %collective-permute-done.19 = f32[16,128]{1,0:T(8,128)S(1)} collective-permute-done((f32[16,128]{1,0:T(8,128)S(1)}, f32[16,128]{1,0:T(8,128)S(1)}, u32[]{:S(2)}, u32[]{:S(2)}) %collective-permute-start.19) | collective-permute-done | bytes 8224 | tf_op jit(solution)/shard_map/ppermute | solution.py:442
  75.1 3.9 %collective-permute-start.20 = (f32[16,128]{1,0:T(8,128)S(1)}, f32[16,128]{1,0:T(8,128)S(1)}, u32[]{:S(2)}, u32[]{:S(2)}) collective-permute-start(f32[16,128]{1,0:T(8,128)S(1)} %add.114), channel_id=1, source_target_pairs={{0,64},{16,80},{32,96},{48,112},{64,0},{80,16},{96,32},{112,48},{1... | collective-permute-start | bytes 24584 | tf_op jit(solution)/shard_map/ppermute | solution.py:442
  78.9 1.6 %collective-permute-done.20 = f32[16,128]{1,0:T(8,128)S(1)} collective-permute-done((f32[16,128]{1,0:T(8,128)S(1)}, f32[16,128]{1,0:T(8,128)S(1)}, u32[]{:S(2)}, u32[]{:S(2)}) %collective-permute-start.20) | collective-permute-done | bytes 8224 | tf_op jit(solution)/shard_map/ppermute | solution.py:442
  80.6 2.5 %collective-permute-start.21 = (f32[16,128]{1,0:T(8,128)S(1)}, f32[16,128]{1,0:T(8,128)S(1)}, u32[]{:S(2)}, u32[]{:S(2)}) collective-permute-start(f32[16,128]{1,0:T(8,128)S(1)} %add.115), channel_id=1, source_target_pairs={{0,1},{1,0},{2,3},{3,2},{4,5},{5,4},{6,7},{7,6},{8,9},{9,8},{10,11... | collective-permute-start | bytes 24584 | tf_op jit(solution)/shard_map/ppermute | solution.py:442
  84.7 4.5 %collective-permute-start.22 = (f32[16,128]{1,0:T(8,128)S(1)}, f32[16,128]{1,0:T(8,128)S(1)}, u32[]{:S(2)}, u32[]{:S(2)}) collective-permute-start(f32[16,128]{1,0:T(8,128)S(1)} %add.116), channel_id=1, source_target_pairs={{0,2},{1,3},{2,0},{3,1},{4,6},{5,7},{6,4},{7,5},{8,10},{9,11},{10,... | collective-permute-start | bytes 24584 | tf_op jit(solution)/shard_map/ppermute | solution.py:442
  89.2 2.0 %broadcast_in_dim.20.spread = f32[128,112,128]{2,1,0:T(8,128)S(1)} broadcast(f32[128,112]{1,0:T(8,128)S(1)} %copy.24), dimensions={0,1} | broadcast | bytes 7397376 | tf_op jit(solution)/shard_map/broadcast_in_dim | solution.py:453
  91.4 12.3 %fluxes.9.rest_0_ = f32[16,128,128]{2,1,0:T(8,128)} custom-call(s32[16]{0:T(128)S(1)} %copy-done.12, f32[16,128,128]{2,1,0:T(8,128)S(1)} %copy-done.4, f32[16,128,128]{2,1,0:T(8,128)S(1)} %copy-done.5, f32[16,1,128]{2,1,0:T(1,128)S(1)} %bitcast.15, f32[16,1,128]{2,1,0:T(1,128)S(1)} %bitcast.24, f32[112,128]{1,0:T(8,128)S(1)} %bitcast.6, ...), custom_call_target="tpu_custom_call" | custom-call | flops 150994944 | bytes 37748736 | tf_op jit(solution)/shard_map/fluxes/pallas_call | solution.py:379
  103.7 8.7 %fluxes.10.rest_0_ = f32[16,128,128]{2,1,0:T(8,128)} custom-call(s32[16]{0:T(128)S(1)} %copy-done.12, f32[16,128,128]{2,1,0:T(8,128)S(1)} %copy-done.4, f32[16,128,128]{2,1,0:T(8,128)S(1)} %copy-done.5, f32[16,1,128]{2,1,0:T(1,128)S(1)} %bitcast.16, f32[16,1,128]{2,1,0:T(1,128)S(1)} %bitcast.25, ...), custom_call_target="tpu_custom_call", output_to_operand_aliasing={{}: (8, {})} | custom-call | flops 75497472 | bytes 18874368 | tf_op jit(solution)/shard_map/fluxes/pallas_call | solution.py:379
  112.3 3.6 %fluxes.11.rest_0_ = f32[16,128,128]{2,1,0:T(8,128)} custom-call(s32[16]{0:T(128)S(1)} %copy-done.12, f32[16,128,128]{2,1,0:T(8,128)S(1)} %copy-done.4, f32[16,128,128]{2,1,0:T(8,128)S(1)} %copy-done.5, f32[16,1,128]{2,1,0:T(1,128)S(1)} %bitcast.17, f32[16,1,128]{2,1,0:T(1,128)S(1)} %bitcast.26, ...), custom_call_target="tpu_custom_call", output_to_operand_aliasing={{}: (8, {})} | custom-call | flops 25165824 | bytes 6291456 | tf_op jit(solution)/shard_map/fluxes/pallas_call | solution.py:379
  116.0 3.6 %fluxes.12.rest_0_ = f32[16,128,128]{2,1,0:T(8,128)} custom-call(s32[16]{0:T(128)S(1)} %copy-done.12, f32[16,128,128]{2,1,0:T(8,128)S(1)} %copy-done.4, f32[16,128,128]{2,1,0:T(8,128)S(1)} %copy-done.5, f32[16,1,128]{2,1,0:T(1,128)S(1)} %bitcast.18, f32[16,1,128]{2,1,0:T(1,128)S(1)} %bitcast.27, ...), custom_call_target="tpu_custom_call", output_to_operand_aliasing={{}: (8, {})} | custom-call | flops 25165824 | bytes 6291456 | tf_op jit(solution)/shard_map/fluxes/pallas_call | solution.py:379
  119.6 3.6 %fluxes.13.rest_0_ = f32[16,128,128]{2,1,0:T(8,128)} custom-call(s32[16]{0:T(128)S(1)} %copy-done.12, f32[16,128,128]{2,1,0:T(8,128)S(1)} %copy-done.4, f32[16,128,128]{2,1,0:T(8,128)S(1)} %copy-done.5, f32[16,1,128]{2,1,0:T(1,128)S(1)} %bitcast.19, f32[16,1,128]{2,1,0:T(1,128)S(1)} %bitcast.28, ...), custom_call_target="tpu_custom_call", output_to_operand_aliasing={{}: (8, {})} | custom-call | flops 25165824 | bytes 6291456 | tf_op jit(solution)/shard_map/fluxes/pallas_call | solution.py:379
  123.2 6.9 %collective-permute-start.24 = (f32[16,128]{1,0:T(8,128)S(1)}, f32[16,128]{1,0:T(8,128)S(1)}, u32[]{:S(2)}, u32[]{:S(2)}) collective-permute-start(f32[16,128]{1,0:T(8,128)S(1)} %add.118), channel_id=1, source_target_pairs={{0,8},{1,9},{2,10},{3,11},{4,12},{5,13},{6,14},{7,15},{8,0},{9,1},... | collective-permute-start | bytes 24584 | tf_op jit(solution)/shard_map/ppermute | solution.py:442
  130.1 3.6 %fluxes.14.rest_0_ = f32[16,128,128]{2,1,0:T(8,128)} custom-call(s32[16]{0:T(128)S(1)} %copy-done.12, f32[16,128,128]{2,1,0:T(8,128)S(1)} %copy-done.4, f32[16,128,128]{2,1,0:T(8,128)S(1)} %copy-done.5, f32[16,1,128]{2,1,0:T(1,128)S(1)} %bitcast.20, f32[16,1,128]{2,1,0:T(1,128)S(1)} %bitcast.29, ...), custom_call_target="tpu_custom_call", output_to_operand_aliasing={{}: (8, {})} | custom-call | flops 25165824 | bytes 6291456 | tf_op jit(solution)/shard_map/fluxes/pallas_call | solution.py:379
  136.5 3.1 %copy-done.1 = f32[128,112,128]{2,1,0:T(8,128)S(1)} copy-done((f32[128,112,128]{2,1,0:T(8,128)S(1)}, f32[128,112,128]{2,1,0:T(8,128)}, u32[]{:S(2)}) %copy-start.1) | copy-done | bytes 7340056
  139.6 3.6 %fluxes.15.rest_0_ = f32[16,128,128]{2,1,0:T(8,128)} custom-call(s32[16]{0:T(128)S(1)} %copy-done.12, f32[16,128,128]{2,1,0:T(8,128)S(1)} %copy-done.4, f32[16,128,128]{2,1,0:T(8,128)S(1)} %copy-done.5, f32[16,1,128]{2,1,0:T(1,128)S(1)} %bitcast.21, f32[16,1,128]{2,1,0:T(1,128)S(1)} %bitcast.30, ...), custom_call_target="tpu_custom_call", output_to_operand_aliasing={{}: (8, {})} | custom-call | flops 25165824 | bytes 6291456 | tf_op jit(solution)/shard_map/fluxes/pallas_call | solution.py:379
  143.3 3.6 %fluxes.16.rest_0_ = f32[16,128,128]{2,1,0:T(8,128)} custom-call(s32[16]{0:T(128)S(1)} %copy-done.12, f32[16,128,128]{2,1,0:T(8,128)S(1)} %copy-done.4, f32[16,128,128]{2,1,0:T(8,128)S(1)} %copy-done.5, f32[16,1,128]{2,1,0:T(1,128)S(1)} %bitcast.22, f32[16,1,128]{2,1,0:T(1,128)S(1)} %bitcast.31, ...), custom_call_target="tpu_custom_call", output_to_operand_aliasing={{}: (8, {})} | custom-call | flops 25165824 | bytes 6291456 | tf_op jit(solution)/shard_map/fluxes/pallas_call | solution.py:379
  146.9 3.6 %fluxes.17 = f32[16,128,128]{2,1,0:T(8,128)} custom-call(s32[16]{0:T(128)S(1)} %copy-done.12, f32[16,128,128]{2,1,0:T(8,128)S(1)} %copy-done.4, f32[16,128,128]{2,1,0:T(8,128)S(1)} %copy-done.5, f32[16,1,128]{2,1,0:T(1,128)S(1)} %bitcast.23, f32[16,1,128]{2,1,0:T(1,128)S(1)} %bitcast.32, f32[112,128]{1,0:T(8,128)S(1)} %bitcast.14, ...), custom_call_target="tpu_custom_call", output_to_operand_aliasing={{}: (8, {})} | custom-call | flops 25165824 | bytes 6291456 | tf_op jit(solution)/shard_map/fluxes/pallas_call | solution.py:379
  150.6 1.9 %recombine.1 = (f32[16,128,128]{2,1,0:T(8,128)S(1)}, f32[16,128,128]{2,1,0:T(8,128)S(1)}, f32[8,128]{1,0:T(8,128)S(1)}) custom-call(f32[16,128]{1,0:T(8,128)S(1)} %add.119.moments, f32[16,128,128]{2,1,0:T(8,128)S(1)} %copy-done.4, f32[6,16,128,128]{3,2,1,0:T(8,128)S(1)} %bitcast.5), custom_call_target="tpu_custom_call" | custom-call | flops 6291456 | bytes 9437184 | tf_op jit(solution)/shard_map/recombine/pallas_call | solution.py:306
  156.7 2.6 %copy.25 = f32[16,128,128]{2,1,0:T(8,128)} copy(f32[16,128,128]{1,0,2:T(8,128)} %get-tuple-element.204) | data formatting | bytes 2097152
  159.2 2.5 %copy.26 = f32[16,128,128]{2,1,0:T(8,128)} copy(f32[16,128,128]{1,0,2:T(8,128)} %get-tuple-element.205) | data formatting | bytes 2097152
  (59 shorter events, 14.8 us)
Async XLA Ops:
  0.6 1.2 copy-start.2
  1.9 1.2 copy-start.6
  3.1 88.2 %copy-start.16 = (f32[112]{0:T(128)S(1)}, f32[112]{0:T(128)}, u32[]{:S(2)}) copy-start(f32[112]{0:T(128)} %param.18) | copy-start | bytes 1348
  3.1 88.2 %copy-start.4 = (f32[16,128,128]{2,1,0:T(8,128)S(1)}, f32[16,128,128]{2,1,0:T(8,128)}, u32[]{:S(2)}) copy-start(f32[16,128,128]{2,1,0:T(8,128)} %state.23) | copy-start | bytes 3145732
  3.1 88.2 %copy-start.5 = (f32[16,128,128]{2,1,0:T(8,128)S(1)}, f32[16,128,128]{2,1,0:T(8,128)}, u32[]{:S(2)}) copy-start(f32[16,128,128]{2,1,0:T(8,128)} %vapour.17) | copy-start | bytes 3145732
  3.1 88.3 %copy-start.9 = (f32[128,112]{0,1:T(8,128)S(1)}, f32[128,112]{0,1:T(8,128)}, u32[]{:S(2)}) copy-start(f32[128,112]{0,1:T(8,128)} %param.17) | copy-start | bytes 172036
  3.1 88.3 %copy-start.10 = (f32[16,128]{1,0:T(8,128)S(1)}, f32[16,128]{1,0:T(8,128)}, u32[]{:S(2)}) copy-start(f32[16,128]{1,0:T(8,128)} %param.15) | copy-start | bytes 24580
  3.1 88.3 %copy-start.11 = (f32[16,128]{1,0:T(8,128)S(1)}, f32[16,128]{1,0:T(8,128)}, u32[]{:S(2)}) copy-start(f32[16,128]{1,0:T(8,128)} %param.16) | copy-start | bytes 24580
  3.1 88.3 %copy-start.12 = (s32[16]{0:T(128)S(1)}, s32[16]{0:T(128)}, u32[]{:S(2)}) copy-start(s32[16]{0:T(128)} %mask.17) | copy-start | bytes 196
  4.8 28.9 %collective-permute-start.12 = (f32[12,128,128]{2,1,0:T(8,128)S(1)}, f32[12,128,128]{2,1,0:T(8,128)S(1)}, u32[]{:S(2)}, u32[]{:S(2)}) collective-permute-start(f32[12,128,128]{2,1,0:T(8,128)S(1)} %get-tuple-element.188), channel_id=1, source_target_pairs={{1,0},{2,1},{3,2},{4,3},{5,4},{6,5},{7,6},{8,7},{9,8},{10,9},{11,1... | collective-permute-start | bytes 2359304 | tf_op jit(solution)/shard_map/ppermute | solution.py:462
  7.2 26.5 %collective-permute-start.13 = (f32[12,128,128]{2,1,0:T(8,128)S(1)}, f32[12,128,128]{2,1,0:T(8,128)S(1)}, u32[]{:S(2)}, u32[]{:S(2)}) collective-permute-start(f32[12,128,128]{2,1,0:T(8,128)S(1)} %get-tuple-element.189), channel_id=1, source_target_pairs={{0,1},{1,2},{2,3},{3,4},{4,5},{5,6},{6,7},{7,8},{8,9},{9,10},{10,1... | collective-permute-start | bytes 2359304 | tf_op jit(solution)/shard_map/ppermute | solution.py:461
  10.7 5.5 %collective-permute-start.14 = (f32[2,128,128]{2,1,0:T(8,128)S(1)}, f32[2,128,128]{2,1,0:T(8,128)S(1)}, u32[]{:S(2)}, u32[]{:S(2)}) collective-permute-start(f32[2,128,128]{2,1,0:T(8,128)S(1)} %get-tuple-element.190), channel_id=1, source_target_pairs={{0,112},{16,0},{32,16},{48,32},{64,48},{80,64},{96,80},{112,96},{1... | collective-permute-start | bytes 393224 | tf_op jit(solution)/shard_map/ppermute | solution.py:459
  13.6 5.6 %collective-permute-start.15 = (f32[2,128,128]{2,1,0:T(8,128)S(1)}, f32[2,128,128]{2,1,0:T(8,128)S(1)}, u32[]{:S(2)}, u32[]{:S(2)}) collective-permute-start(f32[2,128,128]{2,1,0:T(8,128)S(1)} %get-tuple-element.191), channel_id=1, source_target_pairs={{0,16},{16,32},{32,48},{48,64},{64,80},{80,96},{96,112},{112,0},{1... | collective-permute-start | bytes 393224 | tf_op jit(solution)/shard_map/ppermute | solution.py:460
  19.2 12.4 %collective-permute-start.16 = (f32[4,128,128]{2,1,0:T(8,128)S(1)}, f32[4,128,128]{2,1,0:T(8,128)S(1)}, u32[]{:S(2)}, u32[]{:S(2)}) collective-permute-start(f32[4,128,128]{2,1,0:T(8,128)S(1)} %constant_dynamic-update-slice_fusion), channel_id=1, source_target_pairs={{1,0},{2,1},{3,2},{4,3},{5,4},{6,5},{7,6},{8,7},{9,8},{10,9},{11,1... | collective-permute-start | bytes 786440 | tf_op jit(solution)/shard_map/ppermute | solution.py:465
  21.6 12.1 %collective-permute-start.17 = (f32[4,128,128]{2,1,0:T(8,128)S(1)}, f32[4,128,128]{2,1,0:T(8,128)S(1)}, u32[]{:S(2)}, u32[]{:S(2)}) collective-permute-start(f32[4,128,128]{2,1,0:T(8,128)S(1)} %constant_dynamic-update-slice_fusion), channel_id=1, source_target_pairs={{0,1},{1,2},{2,3},{3,4},{4,5},{5,6},{6,7},{7,8},{8,9},{9,10},{10,1... | collective-permute-start | bytes 786440 | tf_op jit(solution)/shard_map/ppermute | solution.py:464
  33.7 1.2 copy-start.3
  34.9 1.2 copy-start.7
  70.2 1.2 collective-permute-start.18
  71.4 3.7 %collective-permute-start.19 = (f32[16,128]{1,0:T(8,128)S(1)}, f32[16,128]{1,0:T(8,128)S(1)}, u32[]{:S(2)}, u32[]{:S(2)}) collective-permute-start(f32[16,128]{1,0:T(8,128)S(1)} %add.113), channel_id=1, source_target_pairs={{0,32},{16,48},{32,0},{48,16},{64,96},{80,112},{96,64},{112,80},{1... | collective-permute-start | bytes 24584 | tf_op jit(solution)/shard_map/ppermute | solution.py:442
  75.1 5.5 %collective-permute-start.20 = (f32[16,128]{1,0:T(8,128)S(1)}, f32[16,128]{1,0:T(8,128)S(1)}, u32[]{:S(2)}, u32[]{:S(2)}) collective-permute-start(f32[16,128]{1,0:T(8,128)S(1)} %add.114), channel_id=1, source_target_pairs={{0,64},{16,80},{32,96},{48,112},{64,0},{80,16},{96,32},{112,48},{1... | collective-permute-start | bytes 24584 | tf_op jit(solution)/shard_map/ppermute | solution.py:442
  80.6 4.1 %collective-permute-start.21 = (f32[16,128]{1,0:T(8,128)S(1)}, f32[16,128]{1,0:T(8,128)S(1)}, u32[]{:S(2)}, u32[]{:S(2)}) collective-permute-start(f32[16,128]{1,0:T(8,128)S(1)} %add.115), channel_id=1, source_target_pairs={{0,1},{1,0},{2,3},{3,2},{4,5},{5,4},{6,7},{7,6},{8,9},{9,8},{10,11... | collective-permute-start | bytes 24584 | tf_op jit(solution)/shard_map/ppermute | solution.py:442
  84.7 19.0 %collective-permute-start.22 = (f32[16,128]{1,0:T(8,128)S(1)}, f32[16,128]{1,0:T(8,128)S(1)}, u32[]{:S(2)}, u32[]{:S(2)}) collective-permute-start(f32[16,128]{1,0:T(8,128)S(1)} %add.116), channel_id=1, source_target_pairs={{0,2},{1,3},{2,0},{3,1},{4,6},{5,7},{6,4},{7,5},{8,10},{9,11},{10,... | collective-permute-start | bytes 24584 | tf_op jit(solution)/shard_map/ppermute | solution.py:442
  91.2 38.9 %copy-start = (f32[128,112,128]{2,1,0:T(8,128)}, f32[128,112,128]{2,1,0:T(8,128)S(1)}, u32[]{:S(2)}) copy-start(f32[128,112,128]{2,1,0:T(8,128)S(1)} %broadcast_in_dim.20.spread) | copy-start | bytes 22020100
  103.6 19.6 %collective-permute-start.23 = (f32[16,128]{1,0:T(8,128)S(1)}, f32[16,128]{1,0:T(8,128)S(1)}, u32[]{:S(2)}, u32[]{:S(2)}) collective-permute-start(f32[16,128]{1,0:T(8,128)S(1)} %add.117), channel_id=1, source_target_pairs={{0,4},{1,5},{2,6},{3,7},{4,0},{5,1},{6,2},{7,3},{8,12},{9,13},{10,... | collective-permute-start | bytes 24584 | tf_op jit(solution)/shard_map/ppermute | solution.py:442
  123.2 10.5 %copy-start.8 = (f32[16,128,128]{2,1,0:T(8,128)S(1)}, f32[16,128,128]{2,1,0:T(8,128)}, u32[]{:S(2)}) copy-start(f32[16,128,128]{2,1,0:T(8,128)} %diff.3) | copy-start | bytes 3145732
  123.2 27.3 %collective-permute-start.24 = (f32[16,128]{1,0:T(8,128)S(1)}, f32[16,128]{1,0:T(8,128)S(1)}, u32[]{:S(2)}, u32[]{:S(2)}) collective-permute-start(f32[16,128]{1,0:T(8,128)S(1)} %add.118), channel_id=1, source_target_pairs={{0,8},{1,9},{2,10},{3,11},{4,12},{5,13},{6,14},{7,15},{8,0},{9,1},... | collective-permute-start | bytes 24584 | tf_op jit(solution)/shard_map/ppermute | solution.py:442
  136.5 3.1 %copy-start.1 = (f32[128,112,128]{2,1,0:T(8,128)S(1)}, f32[128,112,128]{2,1,0:T(8,128)}, u32[]{:S(2)}) copy-start(f32[128,112,128]{2,1,0:T(8,128)} %copy-done) | copy-start | bytes 22020100
  143.3 7.3 %slice-start = ((s8[6291456]{0:T(1024)(128)(4,1)}), s8[4194304]{0:T(1024)(128)(4,1)S(1)}, s32[]{:S(2)}) async-start(s8[6291456]{0:T(1024)(128)(4,1)} %bitcast.4), calls=%async_computation | async-start | bytes 8388608
  146.9 3.7 %slice-start.1 = ((s8[6291456]{0:T(1024)(128)(4,1)}), s8[2097152]{0:T(1024)(128)(4,1)S(1)}, s32[]{:S(2)}) async-start(s8[6291456]{0:T(1024)(128)(4,1)} %bitcast.4), calls=%async_computation.1 | async-start | bytes 4194304

commit v2 on v1

v2 whole, which is shorter than its diff:
```python
import functools
import math

import jax
import jax.numpy as jnp
from jax import lax
from jax.experimental import pallas as pl
from jax.experimental.pallas import tpu as pltpu
from jax.sharding import PartitionSpec as P

ITERS = 5
DEPTH = ITERS + 1
SLOT = 16
GROUP = 8
CHUNK = 32
CENTRE = 14.0
HALF = 13.0
TRUST = 500.0
LOG2E = math.log2(math.e)
GX, GY = ("gx", "gy")
F32 = jnp.float32


def ring(axis, step):
    n = lax.axis_size(axis)
    return [(i, (i + step) % n) for i in range(n)]


def line(axis, step):
    n = lax.axis_size(axis)
    return [(i, i + step) for i in range(n) if 0 <= i + step < n]


def lanes(shape):
    return lax.broadcasted_iota(jnp.int32, shape, len(shape) - 1)


def edges_kernel(state, diff, north, south, east, west):
    rows, levels, width = state.shape
    for f, source in enumerate((state, diff)):

        @pl.loop(0, levels // CHUNK)
        def _(c):
            at = pl.ds(pl.multiple_of(c * CHUNK, CHUNK), CHUNK)
            lane = lanes((CHUNK, width))
            for h, first in enumerate(block_rows(rows)):
                to_west = jnp.zeros((CHUNK, width), F32)
                to_east = jnp.zeros((CHUNK, width), F32)
                for i in range(GROUP):
                    r = first + i
                    if -DEPTH <= r < 0:
                        x = south[f * DEPTH + DEPTH + r, at, :]
                    elif 0 <= r < rows:
                        x = source[r, at, :]
                    elif rows <= r < rows + DEPTH:
                        x = north[f * DEPTH + r - rows, at, :]
                    else:
                        continue
                    place = i * SLOT + DEPTH
                    mine = (lane >= place) & (lane < place + DEPTH)
                    to_west = jnp.where(mine, pltpu.roll(x, place, 1), to_west)
                    place = i * SLOT + 8 - DEPTH
                    mine = (lane >= place) & (lane < place + DEPTH)
                    moved = pltpu.roll(x, (place + DEPTH) % width, 1)
                    to_east = jnp.where(mine, moved, to_east)
                west[h, f, at, :] = to_west
                east[h, f, at, :] = to_east


def block_rows(rows):
    return 0, GROUP, rows, -GROUP


def edges(state, diff, north, south):
    rows, levels, width = state.shape
    thin = jax.ShapeDtypeStruct((4, 2, levels, width), F32)
    return pl.pallas_call(
        edges_kernel,
        out_shape=(thin, thin),
        compiler_params=pltpu.CompilerParams(vmem_limit_bytes=10 << 20),
        cost_estimate=pl.CostEstimate(
            flops=1 << 20, bytes_accessed=4 << 20, transcendentals=0
        ),
        name="edges",
    )(state, diff, north, south)


def basis_kernel(
    state, diff, north, south, east, west, vectors, moments, *work
):
    ce, cw, cn, cl, va, vb, flow, se, sn, sl, sa, sb, sc, joint = work
    rows, levels, width = state.shape
    total = rows + 2 * DEPTH
    tiles = levels // 8
    lane = lanes((8, width))
    in_slot = lane % SLOT

    def sparse(t):
        return pl.ds(t, 8, stride=tiles)

    def root(x):
        return jnp.sqrt(x * (2.0 / HALF))

    def up_level(x):
        return pltpu.roll(x, 7, 0)

    def down_level(x):
        return pltpu.roll(x, 1, 0)

    for f, (own, target) in enumerate(((state, va), (diff, vb))):
        fix = root if f else (lambda x: x)
        for base, source, count in (
            (0, south, DEPTH),
            (DEPTH, own, rows),
            (DEPTH + rows, north, DEPTH),
        ):
            skip = f * DEPTH if count == DEPTH else 0

            @pl.loop(0, count)
            def _(r):
                for t in range(tiles):
                    target[base + r, t] = fix(source[skip + r, sparse(t), :])

    for f, (main, side) in enumerate(((va, sa), (vb, sb))):
        fix = root if f else (lambda x: x)
        for ring_block, base in enumerate(block_rows(rows)):
            first = base + DEPTH

            def strip(t):
                at = sparse(t)
                e, w = east[ring_block, f, at, :], west[ring_block, f, at, :]
                e, w = fix(e), fix(w)
                slots = [i for i in range(GROUP) if 0 <= first + i < total]
                x = [main[first + i, t] for i in slots]
                xe = [pltpu.roll(p, i * SLOT + DEPTH, 1) for i, p in zip(slots, x)]
                xw = [pltpu.roll(p, i * SLOT + 8, 1) for i, p in zip(slots, x)]
                for i, p, q in zip(slots, xe, xw):
                    place = i * SLOT
                    e = jnp.where((lane >= place) & (lane < place + DEPTH), p, e)
                    place = i * SLOT + 8
                    w = jnp.where((lane >= place) & (lane < place + DEPTH), q, w)
                return e, w

            @pl.loop(0, tiles // 4)
            def _(turn):
                made = [strip(turn * 4 + n) for n in range(4)]
                for n, (e, w) in enumerate(made):
                    side[0, ring_block, turn * 4 + n] = e
                    side[1, ring_block, turn * 4 + n] = w

    def join(side):
        seventh = in_slot == 7
        for b in range(4):
            for t in range(tiles):
                joint[b, t] = jnp.where(seventh, side[1, b, t], side[0, b, t])

    def beyond(r):
        place = r - DEPTH + 4 * GROUP
        block, shift = (place // GROUP) % 4, (width - 7 - SLOT * (place % GROUP)) % width
        return lambda t: pltpu.roll(joint[block, t], shift, 1)

    at_end, at_start = lane == width - 1, lane == 0

    def eastward(v, j):
        return jnp.where(lane == width - 1, j, pltpu.roll(v, width - 1, 1))

    def westward(v, j):
        return jnp.where(lane == 0, j, pltpu.roll(v, 1, 1))

    def north_of(values):
        moved = [pltpu.roll(v, width - SLOT, 1) for v in values]
        cut = lane >= width - SLOT
        return [jnp.where(cut, moved[(b + 1) % 4], moved[b]) for b in range(4)]

    def south_of(values):
        moved = [pltpu.roll(v, SLOT, 1) for v in values]
        cut = lane < SLOT
        return [jnp.where(cut, moved[(b + 3) % 4], moved[b]) for b in range(4)]

    top = lax.broadcasted_iota(jnp.int32, (8, width), 0) == 7
    join(sb)

    @pl.loop(0, total)
    def _(r):
        outside = beyond(r)
        up_row = jnp.minimum(r + 1, total - 1)
        for t in range(tiles):
            q, j = vb[r, t], outside(t)
            ce[r, t] = q * eastward(q, j)
            cw[r, t] = q * westward(q, j)
            cn[r, t] = q * vb[up_row, t]
            if t + 1 < tiles:
                cl[r, t] = q * vb[r, t + 1]
            else:
                cl[r, t] = jnp.where(top, 0.0, q * up_level(vb[r, 0]))

    for s in range(2):

        for t in range(tiles):
            q = [sb[s, b, t] for b in range(4)]
            for b, n in enumerate(north_of(q)):
                se[s, b, t] = q[b] * pltpu.roll(q[b], width - 1, 1)
                sn[s, b, t] = q[b] * n

        @pl.loop(0, 4)
        def _(b):
            for t in range(tiles):
                q = sb[s, b, t]
                if t + 1 < tiles:
                    sl[s, b, t] = q * sb[s, b, t + 1]
                else:
                    sl[s, b, t] = jnp.where(top, 0.0, q * up_level(sb[s, b, 0]))

    def advanced(k, spread, v, older):
        if k == 0:
            return spread * (-0.5 * HALF)
        if k == 1:
            return 0.5 * spread + ((1.0 - CENTRE) / HALF) * v
        return spread + (2.0 * (1.0 - CENTRE) / HALF) * v - older

    def apply(k, source, older, target):
        last = k == ITERS

        def row(r, sums, own):
            outside = beyond(r)
            sums = list(sums)
            part = tiles // 2
            made = []
            for h in range(0, tiles, part):
                span = range(h, h + part)
                v = [source[r, t] for t in span]
                j = [outside(t) for t in span]
                e = [pltpu.roll(x, width - 1, 1) for x in v]
                w = [pltpu.roll(x, 1, 1) for x in v]
                under = source[r, h - 1] if h else source[r, tiles - 1]
                over = source[r, h + part] if h + part < tiles else up_level(source[r, 0])
                if h:
                    rise = cl[r, h - 1] * (under - v[0])
                else:
                    rise = down_level(cl[r, tiles - 1] * (under - up_level(v[0])))
                above = v[1:] + [over]
                for n, t in enumerate(span):
                    x = v[n]
                    spread = ce[r, t] * (x - jnp.where(at_end, j[n], e[n]))
                    spread += cw[r, t] * (x - jnp.where(at_start, j[n], w[n]))
                    crossing = cn[r, t] * (x - source[r + 1, t])
                    climb = cl[r, t] * (x - above[n])
                    spread += (crossing - flow[t]) + (climb - rise)
                    rise = climb
                    new = advanced(k, spread, x, older[r, t] if k > 1 else None)
                    made.append((t, crossing, new))
                    if own:
                        products = ([] if last else [new * new]) + ([new * x] if k else [])
                        sums = [p + q for p, q in zip(sums, products)]
                for t, crossing, new in made:
                    flow[t] = crossing
                    target[r, t] = new
                made = []
            return tuple(sums)

        for t in range(tiles):
            flow[t] = cn[k, t] * (source[k, t] - source[k + 1, t])

        def halo(r):
            row(r, (), False)

        if not last:
            pl.loop(k + 1, DEPTH)(halo)
        zero = jnp.zeros((8, width), F32)
        start = (zero,) * (1 if k in (0, ITERS) else 2)
        sums = lax.fori_loop(DEPTH, DEPTH + rows, lambda r, c: row(r, c, True), start)
        if not last:
            pl.loop(DEPTH + rows, total - 1 - k)(halo)
        places = ([] if last else [2 * k]) + ([2 * k - 1] if k else [])
        for place, part in zip(places, sums):
            moments[place : place + 1, :] = jnp.sum(part, 0, keepdims=True)

    def apply_sides(k, source, older, target):
        def block(s, t):
            v = [source[s, b, t] for b in range(4)]
            north = north_of(v)
            crossing = [sn[s, b, t] * (x - n) for b, (x, n) in enumerate(zip(v, north))]
            out = [
                se[s, b, t] * (v[b] - pltpu.roll(v[b], width - 1, 1)) for b in range(4)
            ]
            arrived = south_of(crossing)
            made = []
            for b in range(4):
                spread = out[b] - pltpu.roll(out[b], 1, 1) + (crossing[b] - arrived[b])
                if t + 1 < tiles:
                    over = source[s, b, t + 1]
                else:
                    over = up_level(source[s, b, 0])
                if t:
                    rise = sl[s, b, t - 1] * (source[s, b, t - 1] - v[b])
                else:
                    end = tiles - 1
                    rise = down_level(sl[s, b, end] * (source[s, b, end] - up_level(v[b])))
                spread += sl[s, b, t] * (v[b] - over) - rise
                made.append(advanced(k, spread, v[b], older[s, b, t] if k > 1 else None))
            return made

        @pl.loop(0, 2)
        def _(s):
            for h in range(0, tiles, 4):
                made = [block(s, t) for t in range(h, h + 4)]
                for n, blocks in enumerate(made):
                    for b, new in enumerate(blocks):
                        target[s, b, h + n] = new

    moments[...] = jnp.zeros_like(moments)
    fields = [va] + [vectors.at[k] for k in range(DEPTH)]
    sides = (sb, sc, sa)
    for k in range(DEPTH):
        join(sides[(k - 1) % 3])
        apply(k, fields[k], fields[k - 1], fields[k + 1])
        if k < ITERS:
            apply_sides(k, sides[(k - 1) % 3], sides[(k - 2) % 3], sides[k % 3])


def basis(*arrays):
    rows, levels, width = arrays[0].shape
    total = rows + 2 * DEPTH
    tiles = levels // 8
    main = pltpu.VMEM((total, tiles, 8, width), F32)
    side = pltpu.VMEM((2, 4, tiles, 8, width), F32)
    return pl.pallas_call(
        basis_kernel,
        out_shape=(
            jax.ShapeDtypeStruct((DEPTH, total, tiles, 8, width), F32),
            jax.ShapeDtypeStruct((16, width), F32),
        ),
        scratch_shapes=[main] * 6
        + [pltpu.VMEM((tiles, 8, width), F32)]
        + [side] * 6
        + [pltpu.VMEM((4, tiles, 8, width), F32)],
        out_specs=(
            pl.BlockSpec(memory_space=pltpu.VMEM),
            pl.BlockSpec(memory_space=pltpu.VMEM),
        ),
        compiler_params=pltpu.CompilerParams(vmem_limit_bytes=34 << 20),
        cost_estimate=pl.CostEstimate(
            flops=100 << 20, bytes_accessed=14 << 20, transcendentals=0
        ),
        name="basis",
    )(*arrays)


def coefficients(sums):
    zero = jnp.zeros_like(sums[0])
    one = zero + 1.0
    mom = []
    for k in range(ITERS):
        mom.append(2.0 * sums[2 * k] - (mom[0] if k else sums[0]))
        mom.append(2.0 * sums[2 * k + 1] - (mom[1] if k else sums[1]))

    gram = {}
    for j in range(DEPTH):
        for k in range(j, DEPTH):
            if j + k < 2 * ITERS:
                gram[j, k] = gram[k, j] = 0.5 * (mom[j + k] + mom[k - j])

    def inner(a, b):
        value = size = zero
        for j, p in enumerate(a):
            for k, q in enumerate(b):
                term = p * q * gram[j, k]
                value, size = value + term, size + jnp.abs(term)
        return value, size

    def image(p):
        out = [CENTRE * q for q in p] + [zero]
        for k, q in enumerate(p):
            if k == 0:
                out[1] = out[1] + HALF * q
            else:
                out[k - 1] = out[k - 1] + 0.5 * HALF * q
                out[k + 1] = out[k + 1] + 0.5 * HALF * q
        return out

    def combined(a, scale, b):
        n = max(len(a), len(b))
        a, b = [list(x) + [zero] * (n - len(x)) for x in (a, b)]
        return [p + scale * q for p, q in zip(a, b)]

    residual, direction, field = [one], [one], []
    current, loss = mom[0], one
    for k in range(ITERS):
        applied = image(direction)
        curvature, size = inner(direction, applied)
        loss = jnp.maximum(loss, jnp.where(size < TRUST * curvature, one, 2.0 * one))
        step = current / curvature
        field = combined(field, step, direction)
        residual = combined(residual, -step, applied)
        if k < ITERS - 1:
            following, size = inner(residual, residual)
            loss = jnp.maximum(loss, jnp.where(size < TRUST * following, one, 2.0 * one))
            direction = combined(residual, following / current, direction)
            current = following
    return field, residual, loss


def recombine_kernel(moments, state, vectors, new_state, residual, loss, weights):
    @pl.when(pl.program_id(0) == 0)
    def _():
        width = moments.shape[1]
        sums = [
            jnp.broadcast_to(jnp.sum(moments[i : i + 1, :], 1, keepdims=True), (8, width))
            for i in range(2 * ITERS)
        ]
        field, rest, bad = coefficients(sums)
        for i, value in enumerate(field + rest):
            weights[i] = value
        loss[...] = bad

    count = new_state.shape[0]
    tiles = state.shape[1] // 8
    for n in range(count):
        j = pl.program_id(0) * count + n
        for i in range(tiles):
            at = slice(8 * i, 8 * i + 8)
            ordered = pl.ds((8 * i) % tiles * 8 + 8 * i // tiles, 8, stride=8)
            x, r = state[j, at, :], None
            for k in range(DEPTH):
                v = vectors[k, DEPTH + j, ordered, :]
                if k < ITERS:
                    x = x + weights[k] * v
                part = weights[ITERS + k] * v
                r = part if r is None else r + part
            new_state[n, at, :] = x
            residual[n, at, :] = r


def recombine(moments, state, vectors):
    rows, levels, width = state.shape
    block = pl.BlockSpec((4, levels, width), lambda j: (j, 0, 0))
    resident = pl.BlockSpec(memory_space=pltpu.VMEM)
    vectors = vectors.reshape(*vectors.shape[:2], levels, width)
    whole = lambda *s: pl.BlockSpec(s, lambda j: (0,) * len(s))
    like = jax.ShapeDtypeStruct(state.shape, F32)
    return pl.pallas_call(
        recombine_kernel,
        grid=(rows // 4,),
        out_shape=(like, like, jax.ShapeDtypeStruct((8, width), F32)),
        in_specs=[resident] * 3,
        out_specs=(block, block, whole(8, width)),
        scratch_shapes=[pltpu.VMEM((ITERS + DEPTH, 8, width), F32)],
        compiler_params=pltpu.CompilerParams(vmem_limit_bytes=16 << 20),
        cost_estimate=pl.CostEstimate(
            flops=6 << 20, bytes_accessed=9 << 20, transcendentals=0
        ),
        name="recombine",
    )(moments, state, vectors)


def widened_kernel(eights, spread):
    count, g, _ = eights.shape

    @pl.loop(0, count)
    def _(i):
        columns = eights[i]
        for k in range(8):
            spread[i * 8 + k] = jnp.broadcast_to(columns[:, k : k + 1], spread.shape[1:])


def widened(eights, width):
    count, g, _ = eights.shape
    return pl.pallas_call(
        widened_kernel,
        out_shape=pltpu.VMEM((count * 8, g, width), F32),
        compiler_params=pltpu.CompilerParams(vmem_limit_bytes=11 << 20),
        cost_estimate=pl.CostEstimate(
            flops=2 << 20, bytes_accessed=8 << 20, transcendentals=0
        ),
        name="widened",
    )(eights)


def flux_kernel(first, mask, state, vapour, cosine, albedo, across, spread, weight, *rest):
    out, slanted, upright = rest[-3:]
    levels = state.shape[1]
    tiles = across.shape[0] // 8

    def sunlit(j):
        optical = vapour[j] * (1.0 + 0.5 * jnp.tanh(state[j]))
        mu = cosine[pl.ds(j, 1), :]
        slant = LOG2E / mu
        slanted[...] = optical * -slant
        upright[...] = optical * (1.66 * LOG2E)
        total = jnp.dot(
            across[...], optical, precision=lax.Precision.HIGHEST, preferred_element_type=F32
        )
        down = jnp.log2(weight[...] * mu)
        up = down + jnp.log2(albedo[pl.ds(j, 1), :]) - total * (slant + 1.66 * LOG2E)
        sub = lax.broadcasted_iota(jnp.int32, (8, 128), 0)
        cut = lambda x: tuple(x[8 * t : 8 * t + 8] for t in range(tiles))

        def eight_levels(i, carry):
            down, up = (list(c) for c in carry)
            result = jnp.zeros((8, 128), F32)
            for k in range(8):
                level = i * 8 + k
                o1 = jnp.broadcast_to(slanted[pl.ds(level, 1), :], (8, 128))
                o2 = jnp.broadcast_to(upright[pl.ds(level, 1), :], (8, 128))
                net = None
                for t in range(tiles):
                    a = spread[level, 8 * t : 8 * t + 8, :]
                    down[t] = down[t] + a * o1
                    up[t] = up[t] + a * o2
                    one = jnp.exp2(down[t]) - jnp.exp2(up[t])
                    net = one if net is None else net + one
                result = jnp.where(sub == k, jnp.sum(net, 0, keepdims=True), result)
            out[0, pl.ds(pl.multiple_of(i * 8, 8), 8), :] = result
            return tuple(down), tuple(up)

        lax.fori_loop(0, levels // 8, eight_levels, (cut(down), cut(up)))

    j = first + pl.program_id(0)

    @pl.when(mask[j] == 0)
    def _():
        out[...] = jnp.zeros(out.shape, F32)

    @pl.when(mask[j] != 0)
    def _():
        sunlit(j)


def fluxes(first, count, mask, fields, tables, before):
    state = fields[0]
    rows, levels, width = state.shape
    resident = pl.BlockSpec(memory_space=pltpu.VMEM)
    held = () if before is None else (before,)
    return pl.pallas_call(
        functools.partial(flux_kernel, first),
        out_shape=jax.ShapeDtypeStruct(state.shape, F32),
        grid=(count,),
        in_specs=[pl.BlockSpec(memory_space=pltpu.SMEM)]
        + [resident] * 7
        + [pl.BlockSpec(memory_space=pl.ANY)] * len(held),
        out_specs=pl.BlockSpec((1, levels, width), lambda j: (first + j, 0, 0)),
        scratch_shapes=[pltpu.VMEM((levels, width), F32)] * 2,
        input_output_aliases={8: 0} if held else {},
        compiler_params=pltpu.CompilerParams(vmem_limit_bytes=5 << 20),
        cost_estimate=pl.CostEstimate(
            flops=count * (24 << 20), bytes_accessed=count * (6 << 20), transcendentals=count * (4 << 20)
        ),
        name="fluxes",
    )(mask, *fields, *tables, *held)


def shifted(values):
    width = values.shape[2]
    west = lax.ppermute(values[:, :, width - 1 :], GX, ring(GX, 1))
    east = lax.ppermute(values[:, :, :1], GX, ring(GX, -1))
    south = lax.ppermute(values[-1:], GY, line(GY, 1))
    north = lax.ppermute(values[:1], GY, line(GY, -1))
    wide = jnp.concatenate([west, values, east], 2)
    tall = jnp.concatenate([south, values, north], 0)
    return wide, tall


def plain(state, diff):
    wide, tall = shifted(diff)
    faces = [diff * wide[:, :, 2:], diff * wide[:, :, :-2], diff * tall[2:], diff * tall[:-2]]
    east, west, north, south = [jnp.sqrt(f) for f in faces]
    level = jnp.sqrt(diff[:, 1:] * diff[:, :-1])

    def operate(v):
        wide, tall = shifted(v)
        out = v + east * (v - wide[:, :, 2:]) + west * (v - wide[:, :, :-2])
        out = out + north * (v - tall[2:]) + south * (v - tall[:-2])
        flux = level * (v[:, 1:] - v[:, :-1])
        return out - jnp.pad(flux, ((0, 0), (0, 1), (0, 0))) + jnp.pad(flux, ((0, 0), (1, 0), (0, 0)))

    total = lambda a, b: lax.psum(lax.psum(jnp.sum(a * b), GX), GY)
    residual = state - operate(state)

    def iteration(_, carry):
        field, residual, direction, current = carry
        applied = operate(direction)
        step = current / total(direction, applied)
        field = field + step * direction
        residual = residual - step * applied
        following = total(residual, residual)
        return field, residual, residual + following / current * direction, following

    start = (state, residual, residual, total(residual, residual))
    return lax.fori_loop(0, ITERS, iteration, start)[:2]


def copy_kernel(x, y):
    y[...] = x[...]


def row_major(x):
    return pl.pallas_call(
        copy_kernel, out_shape=jax.ShapeDtypeStruct(x.shape, x.dtype), name="row_major"
    )(x)


def exchanged(part, axis, distances):
    n = lax.axis_size(axis)
    return [part] + [
        lax.ppermute(part, axis, [(i, i ^ d) for i in range(n)]) for d in distances
    ]


def added(parts):
    while len(parts) > 1:
        parts = [a + b for a, b in zip(parts[::2], parts[1::2])]
    return parts[0]


def body(state, diff, vapour, cosine, albedo, absorption, weight, mask):
    rows, levels, width = state.shape
    g = absorption.shape[1]
    eights = jnp.transpose(absorption.reshape(levels // 8, 8, g), (0, 2, 1))
    tables = (
        absorption.T,
        widened(eights, width),
        jnp.broadcast_to(weight[:, None], (g, width)),
    )
    fields = (state, vapour, cosine, albedo)
    after = lax.optimization_barrier

    def both(rows):
        return jnp.concatenate([state[rows], diff[rows]], 0)

    south = lax.ppermute(both(slice(rows - DEPTH, rows)), GY, line(GY, 1))
    north = lax.ppermute(both(slice(0, DEPTH)), GY, line(GY, -1))
    net = fluxes(0, 5, mask, fields, tables, None)
    south, north, net = after((south, north, net))
    to_east, to_west = edges(state, diff, north, south)
    east = lax.ppermute(to_west, GX, ring(GX, -1))
    west = lax.ppermute(to_east, GX, ring(GX, 1))
    net = fluxes(5, 3, mask, fields, tables, net)
    east, west, net = after((east, west, net))
    vectors, moments = basis(state, diff, north, south, east, west)
    first = 8
    stages = ((GX, (1,), 1), (GX, (2, 4, 6), 2), (GY, (1, 2, 3), 2), (GY, (4, 8, 12), 3))
    for axis, distances, count in stages:
        moments, net = after((moments, net))
        parts = exchanged(moments, axis, distances)
        net = fluxes(first, count, mask, fields, tables, net)
        first += count
        parts, net = after((parts, net))
        moments = added(parts)
    new_state, residual, loss = recombine(moments, state, vectors)

    def untrusted(carry):
        return jnp.logical_not(carry[2] <= 1.0)

    def redo(carry):
        again = plain(row_major(state), row_major(diff))
        return (*map(row_major, again), jnp.ones((), F32))

    new_state, residual, _ = lax.while_loop(
        untrusted, redo, (new_state, residual, loss[0, 0])
    )
    return new_state, residual, net


def solution(mesh):
    block = P(GY, None, GX)
    in_specs = (block, block, block, P(GY, GX), P(GY, GX), P(), P(), P((GX, GY)))
    return jax.shard_map(
        body, mesh=mesh, in_specs=in_specs, out_specs=(block,) * 3, check_vma=False
    )
```

time: 163 us -> 133 us (0.82)
  the two profiles are of different devices: /device:TPU:18 before, /device:TPU:100 now
where the time goes in v2:
time: 133 us; the launch traced here: 132 us
  Pallas kernels  98.5 us (74%)
  starting transfers between devices  22.7 us (17%)
  local copies, waits for them, and re-layouts  7.04 us (5%)
  other arithmetic  1.9 us (1%)
    pallas_call x6, Pallas kernels, fluxes(): pl.pallas_call(functools.partial(flux_kernel, first), out_shape=jax.Shape...  51.1 us
    pallas_call x1, Pallas kernels, basis(): pl.pallas_call(basis_kernel, out_shape=(jax.ShapeDtypeStruct((DEPTH, tota...  36.4 us
    ppermute x10, starting transfers between devices, exchanged(): lax.ppermute(part, axis, [(i, i ^ d) for i in range(n)])  14.2 us
    ppermute x1, starting transfers between devices, body(): north = lax.ppermute(both(slice(0, DEPTH)), GY, line(GY, -1))  4.45 us
    pallas_call x1, Pallas kernels, edges(): pl.pallas_call(edges_kernel, out_shape=(thin, thin), compiler_params=pltp...  3.97 us
    pallas_call x1, Pallas kernels, recombine(): pl.pallas_call(recombine_kernel, grid=(rows // 4,), out_shape=(like, like...  3.96 us
    ppermute x1, starting transfers between devices, body(): south = lax.ppermute(both(slice(rows - DEPTH, rows)), GY, line(GY, 1))  3.47 us
    pallas_call x1, Pallas kernels, widened(): pl.pallas_call(widened_kernel, out_shape=pltpu.VMEM((count * 8, g, width)...  3.12 us
  transfers between devices with their start and end apart: 14, of which 0 were waited for; matrix products, arithmetic and copies ran while one was open for 3% of the time, Pallas kernels for 41%

profile of v2, /device:TPU:100, one launch (start us, length us, event | category | flops | bytes accessed | tf_op | source)
XLA Modules:
  0.0 132.0 jit_solution(1042371216074890027)
XLA Ops:
  0.7 1.5 %fusion.52 = (f32[6,128,128]{2,1,0:T(8,128)S(1)}, f32[6,128,128]{2,1,0:T(8,128)S(1)}, f32[6,128,128]{2,1,0:T(8,128)S(1)}, f32[6,128,128]{2,1,0:T(8,128)S(1)}) fusion(f32[16,128,128]{2,1,0:T(8,128)} %state.17, f32[16,128,128]{2,1,0:T(8,128)} %diff.3), kind=kLoop, calls=%fused_computation.71 | loop fusion | bytes 3145728 | tf_op jit(solution)/shard_map/slice | solution.py:628
  2.2 0.9 pad_maximum_fusion.12
  3.1 3.5 %collective-permute-start.12 = (f32[12,128,128]{2,1,0:T(8,128)}, f32[12,128,128]{2,1,0:T(8,128)S(1)}, u32[]{:S(2)}, u32[]{:S(2)}) collective-permute-start(f32[12,128,128]{2,1,0:T(8,128)} %pad_maximum_fusion.12), channel_id=1, source_target_pairs={{0,1},{1,2},{2,3},{3,4},{4,5},{5,6},{6,7},{7,8},{8,9},{9,10},{10,1... | collective-permute-start | bytes 2359304 | tf_op jit(solution)/shard_map/ppermute | solution.py:630
  6.6 0.9 pad_maximum_fusion.13
  7.6 4.5 %collective-permute-start.13 = (f32[12,128,128]{2,1,0:T(8,128)}, f32[12,128,128]{2,1,0:T(8,128)S(1)}, u32[]{:S(2)}, u32[]{:S(2)}) collective-permute-start(f32[12,128,128]{2,1,0:T(8,128)} %pad_maximum_fusion.13), channel_id=1, source_target_pairs={{1,0},{2,1},{3,2},{4,3},{5,4},{6,5},{7,6},{8,7},{9,8},{10,9},{11,1... | collective-permute-start | bytes 2359304 | tf_op jit(solution)/shard_map/ppermute | solution.py:631
  12.0 1.6 %copy.36 = f32[128,112]{1,0:T(8,128)} copy(f32[128,112]{0,1:T(8,128)} %param.17) | data formatting | bytes 114688 | tf_op args[5]
  13.6 1.1 copy.37
  14.7 3.1 %widened.1.spread = f32[128,112,128]{2,1,0:T(8,128)S(1)} custom-call(f32[16,112,8]{2,1,0:T(8,128)S(1)} %bitcast.6), custom_call_target="tpu_custom_call" | custom-call | flops 2097152 | bytes 8388608 | tf_op jit(solution)/shard_map/widened/pallas_call | solution.py:468
  17.8 0.7 broadcast_in_dim.2.weight
  18.6 0.8 copy-done.1
  19.4 0.7 copy-done.5
  20.1 14.4 %fluxes.6.rest_0_ = f32[16,128,128]{2,1,0:T(8,128)} custom-call(s32[16]{0:T(128)S(1)} %copy-done.5, f32[16,128,128]{2,1,0:T(8,128)} %state.17, f32[16,128,128]{2,1,0:T(8,128)S(1)} %copy-done, f32[16,128]{1,0:T(8,128)S(1)} %copy-done.3, f32[16,128]{1,0:T(8,128)S(1)} %copy-done.4, f32[112,128]{1,0:T(8,128)S(1)} %bitcast.7, ...), custom_call_target="tpu_custom_call" | custom-call | flops 125829120 | bytes 31457280 | tf_op jit(solution)/shard_map/fluxes/pallas_call | solution.py:534
  34.4 4.0 %edges.1 = (f32[4,2,128,128]{3,2,1,0:T(8,128)S(1)}, f32[4,2,128,128]{3,2,1,0:T(8,128)S(1)}) custom-call(f32[16,128,128]{2,1,0:T(8,128)} %state.17, f32[16,128,128]{2,1,0:T(8,128)} %diff.3, f32[12,128,128]{2,1,0:T(8,128)S(1)} %collective-permute-done.13.north, f32[12,128,128]{2,1,0:T(8,128)S(1)} %collective-permute-done.12.south), custom_call_target="tpu_custom_call" | custom-call | flops 1048576 | bytes 4194304 | tf_op jit(solution)/shard_map/edges/pallas_call | solution.py:77
  38.5 0.5 collective-permute-start.15
  39.0 9.3 %fluxes.7.rest_0_ = f32[16,128,128]{2,1,0:T(8,128)} custom-call(s32[16]{0:T(128)S(1)} %copy-done.6, f32[16,128,128]{2,1,0:T(8,128)} %state.17, f32[16,128,128]{2,1,0:T(8,128)S(1)} %copy-done, f32[16,128]{1,0:T(8,128)S(1)} %copy-done.3, f32[16,128]{1,0:T(8,128)S(1)} %copy-done.4, f32[112,128]{1,0:T(8,128)S(1)} %bitcast.8, ...), custom_call_target="tpu_custom_call", output_to_operand_aliasing={{}: (8, {})} | custom-call | flops 75497472 | bytes 18874368 | tf_op jit(solution)/shard_map/fluxes/pallas_call | solution.py:534
  48.3 36.4 %basis.1 = (f32[6,28,16,8,128]{4,3,2,1,0:T(8,128)S(1)}, f32[16,128]{1,0:T(8,128)S(1)}) custom-call(f32[16,128,128]{2,1,0:T(8,128)} %state.17, f32[16,128,128]{2,1,0:T(8,128)} %diff.3, f32[12,128,128]{2,1,0:T(8,128)S(1)} %collective-permute-done.13.north, f32[12,128,128]{2,1,0:T(8,128)S(1)} %collective-permute-done.12.south, ...), custom_call_target="tpu_custom_call" | custom-call | flops 104857600 | bytes 14680064 | tf_op jit(solution)/shard_map/basis/pallas_call | solution.py:327
  84.7 1.8 %collective-permute-start.16 = (f32[16,128]{1,0:T(8,128)S(1)}, f32[16,128]{1,0:T(8,128)S(1)}, u32[]{:S(2)}, u32[]{:S(2)}) collective-permute-start(f32[16,128]{1,0:T(8,128)S(1)} %get-tuple-element.229), channel_id=1, source_target_pairs={{0,16},{16,0},{32,48},{48,32},{64,80},{80,64},{96,112},{112,96},{1... | collective-permute-start | bytes 24584 | tf_op jit(solution)/shard_map/ppermute | solution.py:605
  86.5 4.3 %fluxes.8.rest_0_ = f32[16,128,128]{2,1,0:T(8,128)} custom-call(s32[16]{0:T(128)S(1)} %copy-done.6, f32[16,128,128]{2,1,0:T(8,128)} %state.17, f32[16,128,128]{2,1,0:T(8,128)S(1)} %copy-done, f32[16,128]{1,0:T(8,128)S(1)} %copy-done.3, f32[16,128]{1,0:T(8,128)S(1)} %copy-done.4, f32[112,128]{1,0:T(8,128)S(1)} %bitcast.9, ...), custom_call_target="tpu_custom_call", output_to_operand_aliasing={{}: (8, {})} | custom-call | flops 25165824 | bytes 6291456 | tf_op jit(solution)/shard_map/fluxes/pallas_call | solution.py:534
  90.9 0.4 collective-permute-start.19
  91.2 3.7 %collective-permute-start.17 = (f32[16,128]{1,0:T(8,128)S(1)}, f32[16,128]{1,0:T(8,128)S(1)}, u32[]{:S(2)}, u32[]{:S(2)}) collective-permute-start(f32[16,128]{1,0:T(8,128)S(1)} %add.122), channel_id=1, source_target_pairs={{0,32},{16,48},{32,0},{48,16},{64,96},{80,112},{96,64},{112,80},{1... | collective-permute-start | bytes 24584 | tf_op jit(solution)/shard_map/ppermute | solution.py:605
  95.0 6.8 %fluxes.9.rest_0_ = f32[16,128,128]{2,1,0:T(8,128)} custom-call(s32[16]{0:T(128)S(1)} %copy-done.6, f32[16,128,128]{2,1,0:T(8,128)} %state.17, f32[16,128,128]{2,1,0:T(8,128)S(1)} %copy-done, f32[16,128]{1,0:T(8,128)S(1)} %copy-done.3, f32[16,128]{1,0:T(8,128)S(1)} %copy-done.4, f32[112,128]{1,0:T(8,128)S(1)} %bitcast.10, ...), custom_call_target="tpu_custom_call", output_to_operand_aliasing={{}: (8, {})} | custom-call | flops 50331648 | bytes 12582912 | tf_op jit(solution)/shard_map/fluxes/pallas_call | solution.py:534
  101.8 1.0 collective-permute-start.22
  102.8 0.6 collective-permute-start.21
  103.4 2.6 %collective-permute-start.20 = (f32[16,128]{1,0:T(8,128)S(1)}, f32[16,128]{1,0:T(8,128)S(1)}, u32[]{:S(2)}, u32[]{:S(2)}) collective-permute-start(f32[16,128]{1,0:T(8,128)S(1)} %add_add_fusion.2), channel_id=1, source_target_pairs={{0,1},{1,0},{2,3},{3,2},{4,5},{5,4},{6,7},{7,6},{8,9},{9,8},{10,11... | collective-permute-start | bytes 24584 | tf_op jit(solution)/shard_map/ppermute | solution.py:605
  106.0 6.8 %fluxes.10.rest_0_ = f32[16,128,128]{2,1,0:T(8,128)} custom-call(s32[16]{0:T(128)S(1)} %copy-done.6, f32[16,128,128]{2,1,0:T(8,128)} %state.17, f32[16,128,128]{2,1,0:T(8,128)S(1)} %copy-done, f32[16,128]{1,0:T(8,128)S(1)} %copy-done.3, f32[16,128]{1,0:T(8,128)S(1)} %copy-done.4, f32[112,128]{1,0:T(8,128)S(1)} %bitcast.11, ...), custom_call_target="tpu_custom_call", output_to_operand_aliasing={{}: (8, {})} | custom-call | flops 50331648 | bytes 12582912 | tf_op jit(solution)/shard_map/fluxes/pallas_call | solution.py:534
  112.9 0.1 collective-permute-start.25
  113.0 3.3 %collective-permute-start.24 = (f32[16,128]{1,0:T(8,128)S(1)}, f32[16,128]{1,0:T(8,128)S(1)}, u32[]{:S(2)}, u32[]{:S(2)}) collective-permute-start(f32[16,128]{1,0:T(8,128)S(1)} %add_add_fusion.1), channel_id=1, source_target_pairs={{0,8},{1,9},{2,10},{3,11},{4,12},{5,13},{6,14},{7,15},{8,0},{9,1},... | collective-permute-start | bytes 24584 | tf_op jit(solution)/shard_map/ppermute | solution.py:605
  116.2 0.8 collective-permute-start.23
  117.0 9.3 %fluxes.11 = f32[16,128,128]{2,1,0:T(8,128)} custom-call(s32[16]{0:T(128)S(1)} %copy-done.6, f32[16,128,128]{2,1,0:T(8,128)} %state.17, f32[16,128,128]{2,1,0:T(8,128)S(1)} %copy-done, f32[16,128]{1,0:T(8,128)S(1)} %copy-done.3, f32[16,128]{1,0:T(8,128)S(1)} %copy-done.4, f32[112,128]{1,0:T(8,128)S(1)} %bitcast.12, ...), custom_call_target="tpu_custom_call", output_to_operand_aliasing={{}: (8, {})} | custom-call | flops 75497472 | bytes 18874368 | tf_op jit(solution)/shard_map/fluxes/pallas_call | solution.py:534
  126.4 4.0 %recombine.1 = (f32[16,128,128]{2,1,0:T(8,128)}, f32[16,128,128]{2,1,0:T(8,128)}, f32[8,128]{1,0:T(8,128)S(1)}) custom-call(f32[16,128]{1,0:T(8,128)S(1)} %add_add_fusion.moments, f32[16,128,128]{2,1,0:T(8,128)} %state.17, f32[6,28,128,128]{3,2,1,0:T(8,128)S(1)} %bitcast.5), custom_call_target="tpu_custom_call" | custom-call | flops 6291456 | bytes 9437184 | tf_op jit(solution)/shard_map/recombine/pallas_call | solution.py:441
  130.4 0.6 slice.161
  131.0 0.9 while.30
  (32 shorter events, 0.1 us)
Async XLA Ops:
  0.6 17.9 %copy-start.4 = (f32[16,128]{1,0:T(8,128)S(1)}, f32[16,128]{1,0:T(8,128)}, u32[]{:S(2)}) copy-start(f32[16,128]{1,0:T(8,128)} %albedo.11) | copy-start | bytes 24580
  0.6 17.9 %copy-start.3 = (f32[16,128]{1,0:T(8,128)S(1)}, f32[16,128]{1,0:T(8,128)}, u32[]{:S(2)}) copy-start(f32[16,128]{1,0:T(8,128)} %cosine.11) | copy-start | bytes 24580
  0.7 17.9 %copy-start = (f32[16,128,128]{2,1,0:T(8,128)S(1)}, f32[16,128,128]{2,1,0:T(8,128)}, u32[]{:S(2)}) copy-start(f32[16,128,128]{2,1,0:T(8,128)} %vapour.11) | copy-start | bytes 3145732
  3.1 31.3 %collective-permute-start.12 = (f32[12,128,128]{2,1,0:T(8,128)}, f32[12,128,128]{2,1,0:T(8,128)S(1)}, u32[]{:S(2)}, u32[]{:S(2)}) collective-permute-start(f32[12,128,128]{2,1,0:T(8,128)} %pad_maximum_fusion.12), channel_id=1, source_target_pairs={{0,1},{1,2},{2,3},{3,4},{4,5},{5,6},{6,7},{7,8},{8,9},{9,10},{10,1... | collective-permute-start | bytes 2359304 | tf_op jit(solution)/shard_map/ppermute | solution.py:630
  7.6 26.9 %collective-permute-start.13 = (f32[12,128,128]{2,1,0:T(8,128)}, f32[12,128,128]{2,1,0:T(8,128)S(1)}, u32[]{:S(2)}, u32[]{:S(2)}) collective-permute-start(f32[12,128,128]{2,1,0:T(8,128)} %pad_maximum_fusion.13), channel_id=1, source_target_pairs={{1,0},{2,1},{3,2},{4,3},{5,4},{6,5},{7,6},{8,7},{9,8},{10,9},{11,1... | collective-permute-start | bytes 2359304 | tf_op jit(solution)/shard_map/ppermute | solution.py:631
  18.6 0.8 copy-start.1
  19.4 0.7 copy-start.5
  20.1 18.9 %copy-start.2 = (f32[128,112]{0,1:T(8,128)S(1)}, f32[128,112]{0,1:T(8,128)}, u32[]{:S(2)}) copy-start(f32[128,112]{0,1:T(8,128)} %param.17) | copy-start | bytes 172036
  20.1 18.9 %copy-start.6 = (s32[16]{0:T(128)S(1)}, s32[16]{0:T(128)}, u32[]{:S(2)}) copy-start(s32[16]{0:T(128)} %mask.11) | copy-start | bytes 196
  38.4 9.9 %collective-permute-start.14 = (f32[4,2,128,128]{3,2,1,0:T(8,128)S(1)}, f32[4,2,128,128]{3,2,1,0:T(8,128)S(1)}, u32[]{:S(2)}, u32[]{:S(2)}) collective-permute-start(f32[4,2,128,128]{3,2,1,0:T(8,128)S(1)} %get-tuple-element.220), channel_id=1, source_target_pairs={{0,112},{16,0},{32,16},{48,32},{64,48},{80,64},{96,80},{112,96},{1... | collective-permute-start | bytes 1572872 | tf_op jit(solution)/shard_map/ppermute | solution.py:635
  38.5 9.9 %collective-permute-start.15 = (f32[4,2,128,128]{3,2,1,0:T(8,128)S(1)}, f32[4,2,128,128]{3,2,1,0:T(8,128)S(1)}, u32[]{:S(2)}, u32[]{:S(2)}) collective-permute-start(f32[4,2,128,128]{3,2,1,0:T(8,128)S(1)} %get-tuple-element.221), channel_id=1, source_target_pairs={{0,16},{16,32},{32,48},{48,64},{64,80},{80,96},{96,112},{112,0},{1... | collective-permute-start | bytes 1572872 | tf_op jit(solution)/shard_map/ppermute | solution.py:636
  84.7 6.1 %collective-permute-start.16 = (f32[16,128]{1,0:T(8,128)S(1)}, f32[16,128]{1,0:T(8,128)S(1)}, u32[]{:S(2)}, u32[]{:S(2)}) collective-permute-start(f32[16,128]{1,0:T(8,128)S(1)} %get-tuple-element.229), channel_id=1, source_target_pairs={{0,16},{16,0},{32,48},{48,32},{64,80},{80,64},{96,112},{112,96},{1... | collective-permute-start | bytes 24584 | tf_op jit(solution)/shard_map/ppermute | solution.py:605
  90.9 10.9 %collective-permute-start.19 = (f32[16,128]{1,0:T(8,128)S(1)}, f32[16,128]{1,0:T(8,128)S(1)}, u32[]{:S(2)}, u32[]{:S(2)}) collective-permute-start(f32[16,128]{1,0:T(8,128)S(1)} %add.122), channel_id=1, source_target_pairs={{0,96},{16,112},{32,64},{48,80},{64,32},{80,48},{96,0},{112,16},{1... | collective-permute-start | bytes 24584 | tf_op jit(solution)/shard_map/ppermute | solution.py:605
  91.2 10.6 %collective-permute-start.18 = (f32[16,128]{1,0:T(8,128)S(1)}, f32[16,128]{1,0:T(8,128)S(1)}, u32[]{:S(2)}, u32[]{:S(2)}) collective-permute-start(f32[16,128]{1,0:T(8,128)S(1)} %add.122), channel_id=1, source_target_pairs={{0,64},{16,80},{32,96},{48,112},{64,0},{80,16},{96,32},{112,48},{1... | collective-permute-start | bytes 24584 | tf_op jit(solution)/shard_map/ppermute | solution.py:605
  91.2 10.6 %collective-permute-start.17 = (f32[16,128]{1,0:T(8,128)S(1)}, f32[16,128]{1,0:T(8,128)S(1)}, u32[]{:S(2)}, u32[]{:S(2)}) collective-permute-start(f32[16,128]{1,0:T(8,128)S(1)} %add.122), channel_id=1, source_target_pairs={{0,32},{16,48},{32,0},{48,16},{64,96},{80,112},{96,64},{112,80},{1... | collective-permute-start | bytes 24584 | tf_op jit(solution)/shard_map/ppermute | solution.py:605
  101.8 11.0 %collective-permute-start.22 = (f32[16,128]{1,0:T(8,128)S(1)}, f32[16,128]{1,0:T(8,128)S(1)}, u32[]{:S(2)}, u32[]{:S(2)}) collective-permute-start(f32[16,128]{1,0:T(8,128)S(1)} %add_add_fusion.2), channel_id=1, source_target_pairs={{0,3},{1,2},{2,1},{3,0},{4,7},{5,6},{6,5},{7,4},{8,11},{9,10},{10,... | collective-permute-start | bytes 24584 | tf_op jit(solution)/shard_map/ppermute | solution.py:605
  102.8 10.0 %collective-permute-start.21 = (f32[16,128]{1,0:T(8,128)S(1)}, f32[16,128]{1,0:T(8,128)S(1)}, u32[]{:S(2)}, u32[]{:S(2)}) collective-permute-start(f32[16,128]{1,0:T(8,128)S(1)} %add_add_fusion.2), channel_id=1, source_target_pairs={{0,2},{1,3},{2,0},{3,1},{4,6},{5,7},{6,4},{7,5},{8,10},{9,11},{10,... | collective-permute-start | bytes 24584 | tf_op jit(solution)/shard_map/ppermute | solution.py:605
  103.4 9.4 %collective-permute-start.20 = (f32[16,128]{1,0:T(8,128)S(1)}, f32[16,128]{1,0:T(8,128)S(1)}, u32[]{:S(2)}, u32[]{:S(2)}) collective-permute-start(f32[16,128]{1,0:T(8,128)S(1)} %add_add_fusion.2), channel_id=1, source_target_pairs={{0,1},{1,0},{2,3},{3,2},{4,5},{5,4},{6,7},{7,6},{8,9},{9,8},{10,11... | collective-permute-start | bytes 24584 | tf_op jit(solution)/shard_map/ppermute | solution.py:605
  112.9 13.5 %collective-permute-start.25 = (f32[16,128]{1,0:T(8,128)S(1)}, f32[16,128]{1,0:T(8,128)S(1)}, u32[]{:S(2)}, u32[]{:S(2)}) collective-permute-start(f32[16,128]{1,0:T(8,128)S(1)} %add_add_fusion.1), channel_id=1, source_target_pairs={{0,12},{1,13},{2,14},{3,15},{4,8},{5,9},{6,10},{7,11},{8,4},{9,5},... | collective-permute-start | bytes 24584 | tf_op jit(solution)/shard_map/ppermute | solution.py:605
  113.0 13.4 %collective-permute-start.24 = (f32[16,128]{1,0:T(8,128)S(1)}, f32[16,128]{1,0:T(8,128)S(1)}, u32[]{:S(2)}, u32[]{:S(2)}) collective-permute-start(f32[16,128]{1,0:T(8,128)S(1)} %add_add_fusion.1), channel_id=1, source_target_pairs={{0,8},{1,9},{2,10},{3,11},{4,12},{5,13},{6,14},{7,15},{8,0},{9,1},... | collective-permute-start | bytes 24584 | tf_op jit(solution)/shard_map/ppermute | solution.py:605
  116.2 10.2 %collective-permute-start.23 = (f32[16,128]{1,0:T(8,128)S(1)}, f32[16,128]{1,0:T(8,128)S(1)}, u32[]{:S(2)}, u32[]{:S(2)}) collective-permute-start(f32[16,128]{1,0:T(8,128)S(1)} %add_add_fusion.1), channel_id=1, source_target_pairs={{0,4},{1,5},{2,6},{3,7},{4,0},{5,1},{6,2},{7,3},{8,12},{9,13},{10,... | collective-permute-start | bytes 24584 | tf_op jit(solution)/shard_map/ppermute | solution.py:605

commit v3 on v2

--- a/solution.py
+++ b/solution.py
@@ -13,6 +13,8 @@
 SLOT = 16
 GROUP = 8
 CHUNK = 32
+SPAN = 4
+ROWS = 8
 CENTRE = 14.0
 HALF = 13.0
 TRUST = 500.0
@@ -35,7 +37,36 @@
     return lax.broadcasted_iota(jnp.int32, shape, len(shape) - 1)
 
 
-def edges_kernel(state, diff, north, south, east, west):
+def rows_kernel(state, diff, north, south, done):
+    rows = state.shape[0]
+    copies = []
+    for f, source in enumerate((state, diff)):
+        to = pl.ds(f * DEPTH, DEPTH)
+        copies.append((source.at[pl.ds(rows - DEPTH, DEPTH)], north.at[to]))
+        copies.append((source.at[pl.ds(0, DEPTH)], south.at[to]))
+    copies = [pltpu.make_async_copy(x, y, done.at[i]) for i, (x, y) in enumerate(copies)]
+    for copy in copies:
+        copy.start()
+    for copy in copies:
+        copy.wait()
+
+
+def outer_rows(state, diff):
+    rows, levels, width = state.shape
+    tall = jax.ShapeDtypeStruct((2 * DEPTH, levels, width), F32)
+    anywhere = pl.BlockSpec(memory_space=pl.ANY)
+    return pl.pallas_call(
+        rows_kernel,
+        out_shape=(tall, tall),
+        in_specs=[anywhere] * 2,
+        out_specs=(pl.BlockSpec(memory_space=pltpu.VMEM),) * 2,
+        scratch_shapes=[pltpu.SemaphoreType.DMA((4,))],
+        compiler_params=pltpu.CompilerParams(vmem_limit_bytes=3 << 20),
+        name="outer_rows",
+    )(state, diff)
+
+
+def edges_kernel(state, diff, north, south, packed):
     rows, levels, width = state.shape
     for f, source in enumerate((state, diff)):
 
@@ -44,8 +75,7 @@
             at = pl.ds(pl.multiple_of(c * CHUNK, CHUNK), CHUNK)
             lane = lanes((CHUNK, width))
             for h, first in enumerate(block_rows(rows)):
-                to_west = jnp.zeros((CHUNK, width), F32)
-                to_east = jnp.zeros((CHUNK, width), F32)
+                both = jnp.zeros((CHUNK, width), F32)
                 for i in range(GROUP):
                     r = first + i
                     if -DEPTH <= r < 0:
@@ -56,15 +86,10 @@
                         x = north[f * DEPTH + r - rows, at, :]
                     else:
                         continue
-                    place = i * SLOT + DEPTH
-                    mine = (lane >= place) & (lane < place + DEPTH)
-                    to_west = jnp.where(mine, pltpu.roll(x, place, 1), to_west)
-                    place = i * SLOT + 8 - DEPTH
-                    mine = (lane >= place) & (lane < place + DEPTH)
-                    moved = pltpu.roll(x, (place + DEPTH) % width, 1)
-                    to_east = jnp.where(mine, moved, to_east)
-                west[h, f, at, :] = to_west
-                east[h, f, at, :] = to_east
+                    place = i * SLOT
+                    mine = (lane >= place) & (lane < place + 2 * DEPTH)
+                    both = jnp.where(mine, pltpu.roll(x, place + DEPTH, 1), both)
+                packed[h, f, at, :] = both
 
 
 def block_rows(rows):
@@ -76,7 +101,7 @@
     thin = jax.ShapeDtypeStruct((4, 2, levels, width), F32)
     return pl.pallas_call(
         edges_kernel,
-        out_shape=(thin, thin),
+        out_shape=thin,
         compiler_params=pltpu.CompilerParams(vmem_limit_bytes=10 << 20),
         cost_estimate=pl.CostEstimate(
             flops=1 << 20, bytes_accessed=4 << 20, transcendentals=0
@@ -86,9 +111,9 @@
 
 
 def basis_kernel(
-    state, diff, north, south, east, west, vectors, moments, *work
+    state, diff, north, south, packed, east, west, vectors, moments, *work
 ):
-    ce, cw, cn, cl, va, vb, flow, se, sn, sl, sa, sb, sc, joint = work
+    ce, cw, cn, cl, va, vb, flow, se, sw, sn, ss, sl, sa, sb, sc, joint = work
     rows, levels, width = state.shape
     total = rows + 2 * DEPTH
     tiles = levels // 8
@@ -121,38 +146,20 @@
                 for t in range(tiles):
                     target[base + r, t] = fix(source[skip + r, sparse(t), :])
 
-    for f, (main, side) in enumerate(((va, sa), (vb, sb))):
+    near = in_slot < DEPTH
+    for f, side in enumerate((sa, sb)):
         fix = root if f else (lambda x: x)
-        for ring_block, base in enumerate(block_rows(rows)):
-            first = base + DEPTH
-
-            def strip(t):
-                at = sparse(t)
-                e, w = east[ring_block, f, at, :], west[ring_block, f, at, :]
-                e, w = fix(e), fix(w)
-                slots = [i for i in range(GROUP) if 0 <= first + i < total]
-                x = [main[first + i, t] for i in slots]
-                xe = [pltpu.roll(p, i * SLOT + DEPTH, 1) for i, p in zip(slots, x)]
-                xw = [pltpu.roll(p, i * SLOT + 8, 1) for i, p in zip(slots, x)]
-                for i, p, q in zip(slots, xe, xw):
-                    place = i * SLOT
-                    e = jnp.where((lane >= place) & (lane < place + DEPTH), p, e)
-                    place = i * SLOT + 8
-                    w = jnp.where((lane >= place) & (lane < place + DEPTH), q, w)
-                return e, w
-
-            @pl.loop(0, tiles // 4)
-            def _(turn):
-                made = [strip(turn * 4 + n) for n in range(4)]
-                for n, (e, w) in enumerate(made):
-                    side[0, ring_block, turn * 4 + n] = e
-                    side[1, ring_block, turn * 4 + n] = w
+        for b in range(4):
+            for t in range(tiles):
+                own = packed[b, f, sparse(t), :]
+                side[0, b, t] = fix(jnp.where(near, own, east[b, f, sparse(t), :]))
+                side[1, b, t] = fix(jnp.where(near, west[b, f, sparse(t), :], own))
 
     def join(side):
         seventh = in_slot == 7
         for b in range(4):
             for t in range(tiles):
-                joint[b, t] = jnp.where(seventh, side[1, b, t], side[0, b, t])
+                joint[b, t] = jnp.where(seventh, pltpu.roll(side[1, b, t], 2, 1), side[0, b, t])
 
     def beyond(r):
         place = r - DEPTH + 4 * GROUP
@@ -180,27 +187,29 @@
     top = lax.broadcasted_iota(jnp.int32, (8, width), 0) == 7
     join(sb)
 
-    @pl.loop(0, total)
-    def _(r):
-        outside = beyond(r)
-        up_row = jnp.minimum(r + 1, total - 1)
-        for t in range(tiles):
-            q, j = vb[r, t], outside(t)
-            ce[r, t] = q * eastward(q, j)
-            cw[r, t] = q * westward(q, j)
-            cn[r, t] = q * vb[up_row, t]
-            if t + 1 < tiles:
-                cl[r, t] = q * vb[r, t + 1]
-            else:
-                cl[r, t] = jnp.where(top, 0.0, q * up_level(vb[r, 0]))
+    @pl.loop(0, total // 4)
+    def _(turn):
+        for r in [turn * 4 + n for n in range(4)]:
+            outside = beyond(r)
+            up_row = jnp.minimum(r + 1, total - 1)
+            q = [vb[r, t] for t in range(tiles)]
+            j = [outside(t) for t in range(tiles)]
+            above = q[1:] + [jnp.where(top, 0.0, up_level(q[0]))]
+            for t in range(tiles):
+                ce[r, t] = q[t] * eastward(q[t], j[t])
+                cw[r, t] = q[t] * westward(q[t], j[t])
+                cn[r, t] = q[t] * vb[up_row, t]
+                cl[r, t] = q[t] * above[t]
 
     for s in range(2):
 
         for t in range(tiles):
             q = [sb[s, b, t] for b in range(4)]
-            for b, n in enumerate(north_of(q)):
+            for b, (n, d) in enumerate(zip(north_of(q), south_of(q))):
                 se[s, b, t] = q[b] * pltpu.roll(q[b], width - 1, 1)
+                sw[s, b, t] = q[b] * pltpu.roll(q[b], 1, 1)
                 sn[s, b, t] = q[b] * n
+                ss[s, b, t] = q[b] * d
 
         @pl.loop(0, 4)
         def _(b):
@@ -221,92 +230,94 @@
     def apply(k, source, older, target):
         last = k == ITERS
 
-        def row(r, sums, own):
-            outside = beyond(r)
+        def several(first, count, sums, own):
             sums = list(sums)
-            part = tiles // 2
-            made = []
-            for h in range(0, tiles, part):
-                span = range(h, h + part)
-                v = [source[r, t] for t in span]
-                j = [outside(t) for t in span]
+            crossed = [flow[t] for t in range(tiles)]
+            for r in [first + n for n in range(count)]:
+                outside = beyond(r)
+                v = [source[r, t] for t in range(tiles)]
+                j = [outside(t) for t in range(tiles)]
                 e = [pltpu.roll(x, width - 1, 1) for x in v]
                 w = [pltpu.roll(x, 1, 1) for x in v]
-                under = source[r, h - 1] if h else source[r, tiles - 1]
-                over = source[r, h + part] if h + part < tiles else up_level(source[r, 0])
-                if h:
-                    rise = cl[r, h - 1] * (under - v[0])
-                else:
-                    rise = down_level(cl[r, tiles - 1] * (under - up_level(v[0])))
-                above = v[1:] + [over]
-                for n, t in enumerate(span):
-                    x = v[n]
-                    spread = ce[r, t] * (x - jnp.where(at_end, j[n], e[n]))
-                    spread += cw[r, t] * (x - jnp.where(at_start, j[n], w[n]))
+                above = v[1:] + [up_level(v[0])]
+                rise = down_level(cl[r, tiles - 1] * (v[-1] - above[-1]))
+                made = []
+                for t, x in enumerate(v):
+                    spread = ce[r, t] * (x - jnp.where(at_end, j[t], e[t]))
+                    spread += cw[r, t] * (x - jnp.where(at_start, j[t], w[t]))
                     crossing = cn[r, t] * (x - source[r + 1, t])
-                    climb = cl[r, t] * (x - above[n])
-                    spread += (crossing - flow[t]) + (climb - rise)
-                    rise = climb
+                    climb = cl[r, t] * (x - above[t])
+                    spread += (crossing - crossed[t]) + (climb - rise)
+                    crossed[t], rise = crossing, climb
                     new = advanced(k, spread, x, older[r, t] if k > 1 else None)
-                    made.append((t, crossing, new))
+                    made.append(new)
                     if own:
                         products = ([] if last else [new * new]) + ([new * x] if k else [])
                         sums = [p + q for p, q in zip(sums, products)]
-                for t, crossing, new in made:
-                    flow[t] = crossing
+                for t, new in enumerate(made):
                     target[r, t] = new
-                made = []
+            for t in range(tiles):
+                flow[t] = crossed[t]
             return tuple(sums)
 
         for t in range(tiles):
             flow[t] = cn[k, t] * (source[k, t] - source[k + 1, t])
 
-        def halo(r):
-            row(r, (), False)
-
         if not last:
-            pl.loop(k + 1, DEPTH)(halo)
+            several(k + 1, DEPTH - k - 1, (), False)
         zero = jnp.zeros((8, width), F32)
         start = (zero,) * (1 if k in (0, ITERS) else 2)
-        sums = lax.fori_loop(DEPTH, DEPTH + rows, lambda r, c: row(r, c, True), start)
+        sums = lax.fori_loop(
+            0,
+            rows // ROWS,
+            lambda n, c: several(DEPTH + n * ROWS, ROWS, c, True),
+            start,
+        )
         if not last:
-            pl.loop(DEPTH + rows, total - 1 - k)(halo)
+            several(DEPTH + rows, DEPTH - k - 1, (), False)
         places = ([] if last else [2 * k]) + ([2 * k - 1] if k else [])
         for place, part in zip(places, sums):
             moments[place : place + 1, :] = jnp.sum(part, 0, keepdims=True)
 
     def apply_sides(k, source, older, target):
-        def block(s, t):
-            v = [source[s, b, t] for b in range(4)]
-            north = north_of(v)
-            crossing = [sn[s, b, t] * (x - n) for b, (x, n) in enumerate(zip(v, north))]
-            out = [
-                se[s, b, t] * (v[b] - pltpu.roll(v[b], width - 1, 1)) for b in range(4)
-            ]
-            arrived = south_of(crossing)
-            made = []
+        def blocks(s, span):
+            v = {(b, t): source[s, b, t] for t in span for b in range(4)}
+            e = {p: pltpu.roll(x, width - 1, 1) for p, x in v.items()}
+            w = {p: pltpu.roll(x, 1, 1) for p, x in v.items()}
+            n, d = {}, {}
+            for t in span:
+                column = [v[b, t] for b in range(4)]
+                for b, (x, y) in enumerate(zip(north_of(column), south_of(column))):
+                    n[b, t], d[b, t] = x, y
+            made = {}
             for b in range(4):
-                spread = out[b] - pltpu.roll(out[b], 1, 1) + (crossing[b] - arrived[b])
-                if t + 1 < tiles:
-                    over = source[s, b, t + 1]
-                else:
-                    over = up_level(source[s, b, 0])
+                t = span[0]
                 if t:
-                    rise = sl[s, b, t - 1] * (source[s, b, t - 1] - v[b])
+                    rise = sl[s, b, t - 1] * (source[s, b, t - 1] - v[b, t])
                 else:
                     end = tiles - 1
-                    rise = down_level(sl[s, b, end] * (source[s, b, end] - up_level(v[b])))
-                spread += sl[s, b, t] * (v[b] - over) - rise
-                made.append(advanced(k, spread, v[b], older[s, b, t] if k > 1 else None))
+                    rise = sl[s, b, end] * (source[s, b, end] - up_level(v[b, t]))
+                    rise = down_level(rise)
+                for t in span:
+                    x = v[b, t]
+                    if t + 1 < tiles:
+                        over = v[b, t + 1] if t + 1 in span else source[s, b, t + 1]
+                    else:
+                        over = up_level(source[s, b, 0])
+                    climb = sl[s, b, t] * (x - over)
+                    spread = se[s, b, t] * (x - e[b, t]) + sw[s, b, t] * (x - w[b, t])
+                    spread += sn[s, b, t] * (x - n[b, t]) + ss[s, b, t] * (x - d[b, t])
+                    spread += climb - rise
+                    rise = climb
+                    last = older[s, b, t] if k > 1 else None
+                    made[b, t] = advanced(k, spread, x, last)
             return made
 
         @pl.loop(0, 2)
         def _(s):
-            for h in range(0, tiles, 4):
-                made = [block(s, t) for t in range(h, h + 4)]
-                for n, blocks in enumerate(made):
-                    for b, new in enumerate(blocks):
-                        target[s, b, h + n] = new
+            for h in range(0, tiles, SPAN):
+                for (b, t), new in blocks(s, range(h, h + SPAN)).items():
+                    target[s, b, t] = new
 
     moments[...] = jnp.zeros_like(moments)
     fields = [va] + [vectors.at[k] for k in range(DEPTH)]
@@ -332,7 +343,7 @@
         ),
         scratch_shapes=[main] * 6
         + [pltpu.VMEM((tiles, 8, width), F32)]
-        + [side] * 6
+        + [side] * 8
         + [pltpu.VMEM((4, tiles, 8, width), F32)],
         out_specs=(
             pl.BlockSpec(memory_space=pltpu.VMEM),
@@ -453,36 +464,46 @@
     )(moments, state, vectors)
 
 
-def widened_kernel(eights, spread):
-    count, g, _ = eights.shape
-
-    @pl.loop(0, count)
-    def _(i):
-        columns = eights[i]
-        for k in range(8):
-            spread[i * 8 + k] = jnp.broadcast_to(columns[:, k : k + 1], spread.shape[1:])
-
-
-def widened(eights, width):
-    count, g, _ = eights.shape
+def tables_kernel(absorption, weight, state, vapour, optical, across, spread, weights):
+    levels, g = absorption.shape
+    width = state.shape[2]
+    turned = jnp.transpose(absorption[...])
+    across[...] = turned
+    weights[...] = jnp.transpose(jnp.broadcast_to(weight[...], (width, g)))
+    for level in range(levels):
+        spread[level] = jnp.broadcast_to(turned[:, level : level + 1], (g, width))
+
+    @pl.loop(0, state.shape[0])
+    def _(r):
+        optical[r] = vapour[r] * (1.0 + 0.5 * jnp.tanh(state[r]))
+
+
+def flux_tables(absorption, weight, state, vapour):
+    rows, levels, width = state.shape
+    g = absorption.shape[1]
     return pl.pallas_call(
-        widened_kernel,
-        out_shape=pltpu.VMEM((count * 8, g, width), F32),
-        compiler_params=pltpu.CompilerParams(vmem_limit_bytes=11 << 20),
+        tables_kernel,
+        out_shape=(
+            pltpu.VMEM(state.shape, F32),
+            pltpu.VMEM((g, levels), F32),
+            pltpu.VMEM((levels, g, width), F32),
+            pltpu.VMEM((g, width), F32),
+        ),
+        compiler_params=pltpu.CompilerParams(vmem_limit_bytes=13 << 20),
         cost_estimate=pl.CostEstimate(
-            flops=2 << 20, bytes_accessed=8 << 20, transcendentals=0
-        ),
-        name="widened",
-    )(eights)
-
-
-def flux_kernel(first, mask, state, vapour, cosine, albedo, across, spread, weight, *rest):
+            flops=2 << 20, bytes_accessed=10 << 20, transcendentals=1 << 18
+        ),
+        name="flux_tables",
+    )(absorption, weight[None], state, vapour)
+
+
+def flux_kernel(first, mask, amounts, cosine, albedo, across, spread, weight, *rest):
     out, slanted, upright = rest[-3:]
-    levels = state.shape[1]
+    levels = amounts.shape[1]
     tiles = across.shape[0] // 8
 
     def sunlit(j):
-        optical = vapour[j] * (1.0 + 0.5 * jnp.tanh(state[j]))
+        optical = amounts[j]
         mu = cosine[pl.ds(j, 1), :]
         slant = LOG2E / mu
         slanted[...] = optical * -slant
@@ -527,20 +548,19 @@
 
 
 def fluxes(first, count, mask, fields, tables, before):
-    state = fields[0]
-    rows, levels, width = state.shape
+    rows, levels, width = fields[0].shape
     resident = pl.BlockSpec(memory_space=pltpu.VMEM)
     held = () if before is None else (before,)
     return pl.pallas_call(
         functools.partial(flux_kernel, first),
-        out_shape=jax.ShapeDtypeStruct(state.shape, F32),
+        out_shape=jax.ShapeDtypeStruct(fields[0].shape, F32),
         grid=(count,),
         in_specs=[pl.BlockSpec(memory_space=pltpu.SMEM)]
-        + [resident] * 7
+        + [resident] * 6
         + [pl.BlockSpec(memory_space=pl.ANY)] * len(held),
         out_specs=pl.BlockSpec((1, levels, width), lambda j: (first + j, 0, 0)),
         scratch_shapes=[pltpu.VMEM((levels, width), F32)] * 2,
-        input_output_aliases={8: 0} if held else {},
+        input_output_aliases={7: 0} if held else {},
         compiler_params=pltpu.CompilerParams(vmem_limit_bytes=5 << 20),
         cost_estimate=pl.CostEstimate(
             flops=count * (24 << 20), bytes_accessed=count * (6 << 20), transcendentals=count * (4 << 20)
@@ -613,30 +633,21 @@
 
 
 def body(state, diff, vapour, cosine, albedo, absorption, weight, mask):
-    rows, levels, width = state.shape
-    g = absorption.shape[1]
-    eights = jnp.transpose(absorption.reshape(levels // 8, 8, g), (0, 2, 1))
-    tables = (
-        absorption.T,
-        widened(eights, width),
-        jnp.broadcast_to(weight[:, None], (g, width)),
-    )
-    fields = (state, vapour, cosine, albedo)
     after = lax.optimization_barrier
 
-    def both(rows):
-        return jnp.concatenate([state[rows], diff[rows]], 0)
-
-    south = lax.ppermute(both(slice(rows - DEPTH, rows)), GY, line(GY, 1))
-    north = lax.ppermute(both(slice(0, DEPTH)), GY, line(GY, -1))
+    to_north, to_south = outer_rows(state, diff)
+    south = lax.ppermute(to_north, GY, line(GY, 1))
+    north = lax.ppermute(to_south, GY, line(GY, -1))
+    optical, *tables = flux_tables(absorption, weight, state, vapour)
+    fields = (optical, cosine, albedo)
     net = fluxes(0, 5, mask, fields, tables, None)
     south, north, net = after((south, north, net))
-    to_east, to_west = edges(state, diff, north, south)
-    east = lax.ppermute(to_west, GX, ring(GX, -1))
-    west = lax.ppermute(to_east, GX, ring(GX, 1))
+    packed = edges(state, diff, north, south)
+    east = lax.ppermute(packed, GX, ring(GX, -1))
+    west = lax.ppermute(packed, GX, ring(GX, 1))
     net = fluxes(5, 3, mask, fields, tables, net)
     east, west, net = after((east, west, net))
-    vectors, moments = basis(state, diff, north, south, east, west)
+    vectors, moments = basis(state, diff, north, south, packed, east, west)
     first = 8
     stages = ((GX, (1,), 1), (GX, (2, 4, 6), 2), (GY, (1, 2, 3), 2), (GY, (4, 8, 12), 3))
     for axis, distances, count in stages:

time: 133 us -> 110 us (0.83)
  Pallas kernels: 98.5 us -> 78.3 us
  other arithmetic: 1.9 us -> 0.03 us
  local copies, waits for them, and re-layouts: 7.04 us -> 5.42 us
    pallas_call x1, Pallas kernels: 36.4 us -> 19.6 us  [basis(): pl.pallas_call(basis_kernel, out_shape=(jax.ShapeDtypeStruct((DEPTH, tota...]
    pallas_call x6, Pallas kernels: 51.1 us -> 46.7 us  [fluxes(): pl.pallas_call(functools.partial(flux_kernel, first), out_shape=jax.Shape...]
    concatenate x2 -> x0, other arithmetic: 1.87 us -> none  [both(): return jnp.concatenate([state[rows], diff[rows]], 0)]
    unnamed x15 -> x17, local copies, waits for them, and re-layouts: 3.04 us -> 4.84 us
    slice x1 -> x0, local copies, waits for them, and re-layouts: 1.55 us -> none  [both(): return jnp.concatenate([state[rows], diff[rows]], 0)]
    ppermute x10, starting transfers between devices: 14.2 us -> 12.7 us  [exchanged(): lax.ppermute(part, axis, [(i, i ^ d) for i in range(n)])]
    pallas_call x2 -> x3, Pallas kernels: 7.09 us -> 8.16 us  [the longest x1 3.76 us: flux_tables(): pl.pallas_call(tables_kernel, out_shape=(pltpu.VMEM(state.shape, F32), pl...]
  transfers between devices with their start and end apart: 14 -> 14, of which waited for: 0 -> 0; matrix products, arithmetic and copies ran while one was open for 3% -> 1% of each run, Pallas kernels for 41% -> 47%
where the time goes in v3:
time: 110 us; the launch traced here: 108 us
  Pallas kernels  78.3 us (71%)
  starting transfers between devices  22.4 us (20%)
  local copies, waits for them, and re-layouts  5.42 us (5%)
    pallas_call x6, Pallas kernels, fluxes(): pl.pallas_call(functools.partial(flux_kernel, first), out_shape=jax.Shape...  46.7 us
    pallas_call x1, Pallas kernels, basis(): pl.pallas_call(basis_kernel, out_shape=(jax.ShapeDtypeStruct((DEPTH, tota...  19.6 us
    ppermute x10, starting transfers between devices, exchanged(): lax.ppermute(part, axis, [(i, i ^ d) for i in range(n)])  12.7 us
    unnamed x17, local copies, waits for them, and re-layouts  4.84 us
    ppermute x1, starting transfers between devices, body(): north = lax.ppermute(to_south, GY, line(GY, -1))  4.47 us
    pallas_call x1, Pallas kernels, recombine(): pl.pallas_call(recombine_kernel, grid=(rows // 4,), out_shape=(like, like...  3.96 us
    pallas_call x1, Pallas kernels, flux_tables(): pl.pallas_call(tables_kernel, out_shape=(pltpu.VMEM(state.shape, F32), pl...  3.76 us
    ppermute x1, starting transfers between devices, body(): south = lax.ppermute(to_north, GY, line(GY, 1))  3.48 us
  transfers between devices with their start and end apart: 14, of which 0 were waited for; matrix products, arithmetic and copies ran while one was open for 1% of the time, Pallas kernels for 47%

profile of v3, /device:TPU:100, one launch (start us, length us, event | category | flops | bytes accessed | tf_op | source)
XLA Modules:
  0.0 108.0 jit_solution(2030445983434398190)
XLA Ops:
  0.6 1.4 %outer_rows.1 = (f32[12,128,128]{2,1,0:T(8,128)S(1)}, f32[12,128,128]{2,1,0:T(8,128)S(1)}) custom-call(f32[16,128,128]{2,1,0:T(8,128)} %state.9, f32[16,128,128]{2,1,0:T(8,128)} %diff.5), custom_call_target="tpu_custom_call" | custom-call | tf_op jit(solution)/shard_map/outer_rows/pallas_call | solution.py:58
  2.0 3.5 %collective-permute-start.12 = (f32[12,128,128]{2,1,0:T(8,128)S(1)}, f32[12,128,128]{2,1,0:T(8,128)S(1)}, u32[]{:S(2)}, u32[]{:S(2)}) collective-permute-start(f32[12,128,128]{2,1,0:T(8,128)S(1)} %get-tuple-element.222), channel_id=1, source_target_pairs={{0,1},{1,2},{2,3},{3,4},{4,5},{5,6},{6,7},{7,8},{8,9},{9,10},{10,1... | collective-permute-start | bytes 2359304 | tf_op jit(solution)/shard_map/ppermute | solution.py:639
  5.5 4.5 %collective-permute-start.13 = (f32[12,128,128]{2,1,0:T(8,128)S(1)}, f32[12,128,128]{2,1,0:T(8,128)S(1)}, u32[]{:S(2)}, u32[]{:S(2)}) collective-permute-start(f32[12,128,128]{2,1,0:T(8,128)S(1)} %get-tuple-element.223), channel_id=1, source_target_pairs={{1,0},{2,1},{3,2},{4,3},{5,4},{6,5},{7,6},{8,7},{9,8},{10,9},{11,1... | collective-permute-start | bytes 2359304 | tf_op jit(solution)/shard_map/ppermute | solution.py:640
  10.0 0.9 copy.35.absorption
  10.9 1.2 %copy-done = f32[16,128,128]{2,1,0:T(8,128)S(1)} copy-done((f32[16,128,128]{2,1,0:T(8,128)S(1)}, f32[16,128,128]{2,1,0:T(8,128)}, u32[]{:S(2)}) %copy-start) | copy-done | bytes 1048600
  12.1 0.7 copy-done.5
  12.8 3.8 %flux_tables.1 = (f32[16,128,128]{2,1,0:T(8,128)S(1)}, f32[112,128]{1,0:T(8,128)S(1)}, f32[128,112,128]{2,1,0:T(8,128)S(1)}, f32[112,128]{1,0:T(8,128)S(1)}) custom-call(f32[128,112]{1,0:T(8,128)S(1)} %copy.35.absorption, f32[1,112]{1,0:T(1,128)S(1)} %bitcast.4, f32[16,128,128]{2,1,0:T(8,128)} %state.9, f32[16,128,128]{2,1,0:T(8,128)S(1)} %copy-done), custom_call_target="tpu_custom_call" | custom-call | flops 2097152 | bytes 10485760 | tf_op jit(solution)/shard_map/flux_tables/pallas_call | solution.py:484
  16.6 0.7 copy-done.1
  17.3 0.7 copy-done.3
  18.0 0.7 copy-done.6
  18.6 13.6 %fluxes.6.rest_0_ = f32[16,128,128]{2,1,0:T(8,128)} custom-call(s32[16]{0:T(128)S(1)} %copy-done.6, f32[16,128,128]{2,1,0:T(8,128)S(1)} %get-tuple-element.224.amounts, f32[16,128]{1,0:T(8,128)S(1)} %copy-done.1, f32[16,128]{1,0:T(8,128)S(1)} %copy-done.3, f32[112,128]{1,0:T(8,128)S(1)} %get-tuple-element.225.across, ...), custom_call_target="tpu_custom_call" | custom-call | flops 125829120 | bytes 31457280 | tf_op jit(solution)/shard_map/fluxes/pallas_call | solution.py:554
  32.2 3.0 %edges.1.packed = f32[4,2,128,128]{3,2,1,0:T(8,128)S(1)} custom-call(f32[16,128,128]{2,1,0:T(8,128)} %state.9, f32[16,128,128]{2,1,0:T(8,128)} %diff.5, f32[12,128,128]{2,1,0:T(8,128)S(1)} %collective-permute-done.13.north, f32[12,128,128]{2,1,0:T(8,128)S(1)} %collective-permute-done.12.south), custom_call_target="tpu_custom_call" | custom-call | flops 1048576 | bytes 4194304 | tf_op jit(solution)/shard_map/edges/pallas_call | solution.py:102
  35.2 0.0 collective-permute-start.15
  35.3 1.7 %collective-permute-start.14 = (f32[4,2,128,128]{3,2,1,0:T(8,128)S(1)}, f32[4,2,128,128]{3,2,1,0:T(8,128)S(1)}, u32[]{:S(2)}, u32[]{:S(2)}) collective-permute-start(f32[4,2,128,128]{3,2,1,0:T(8,128)S(1)} %edges.1.packed), channel_id=1, source_target_pairs={{0,112},{16,0},{32,16},{48,32},{64,48},{80,64},{96,80},{112,96},{1... | collective-permute-start | bytes 1572872 | tf_op jit(solution)/shard_map/ppermute | solution.py:646
  37.0 8.6 %fluxes.7.rest_0_ = f32[16,128,128]{2,1,0:T(8,128)} custom-call(s32[16]{0:T(128)S(1)} %copy-done.7, f32[16,128,128]{2,1,0:T(8,128)S(1)} %get-tuple-element.224.amounts, f32[16,128]{1,0:T(8,128)S(1)} %copy-done.1, f32[16,128]{1,0:T(8,128)S(1)} %copy-done.4, f32[112,128]{1,0:T(8,128)S(1)} %get-tuple-element.225.across, ...), custom_call_target="tpu_custom_call", output_to_operand_aliasing={{}: (7, {})} | custom-call | flops 75497472 | bytes 18874368 | tf_op jit(solution)/shard_map/fluxes/pallas_call | solution.py:554
  45.6 19.6 %basis.1 = (f32[6,28,16,8,128]{4,3,2,1,0:T(8,128)S(1)}, f32[16,128]{1,0:T(8,128)S(1)}) custom-call(f32[16,128,128]{2,1,0:T(8,128)} %state.9, f32[16,128,128]{2,1,0:T(8,128)} %diff.5, f32[12,128,128]{2,1,0:T(8,128)S(1)} %collective-permute-done.13.north, f32[12,128,128]{2,1,0:T(8,128)S(1)} %collective-permute-done.12.south, ...), custom_call_target="tpu_custom_call" | custom-call | flops 104857600 | bytes 14680064 | tf_op jit(solution)/shard_map/basis/pallas_call | solution.py:338
  65.2 0.3 collective-permute-start.16
  65.5 3.6 %fluxes.8.rest_0_ = f32[16,128,128]{2,1,0:T(8,128)} custom-call(s32[16]{0:T(128)S(1)} %copy-done.7, f32[16,128,128]{2,1,0:T(8,128)S(1)} %get-tuple-element.224.amounts, f32[16,128]{1,0:T(8,128)S(1)} %copy-done.2, f32[16,128]{1,0:T(8,128)S(1)} %copy-done.4, f32[112,128]{1,0:T(8,128)S(1)} %get-tuple-element.225.across, ...), custom_call_target="tpu_custom_call", output_to_operand_aliasing={{}: (7, {})} | custom-call | flops 25165824 | bytes 6291456 | tf_op jit(solution)/shard_map/fluxes/pallas_call | solution.py:554
  69.1 0.4 collective-permute-start.19
  69.5 3.7 %collective-permute-start.17 = (f32[16,128]{1,0:T(8,128)S(1)}, f32[16,128]{1,0:T(8,128)S(1)}, u32[]{:S(2)}, u32[]{:S(2)}) collective-permute-start(f32[16,128]{1,0:T(8,128)S(1)} %add.122), channel_id=1, source_target_pairs={{0,32},{16,48},{32,0},{48,16},{64,96},{80,112},{96,64},{112,80},{1... | collective-permute-start | bytes 24584 | tf_op jit(solution)/shard_map/ppermute | solution.py:625
  73.2 6.1 %fluxes.9.rest_0_ = f32[16,128,128]{2,1,0:T(8,128)} custom-call(s32[16]{0:T(128)S(1)} %copy-done.7, f32[16,128,128]{2,1,0:T(8,128)S(1)} %get-tuple-element.224.amounts, f32[16,128]{1,0:T(8,128)S(1)} %copy-done.2, f32[16,128]{1,0:T(8,128)S(1)} %copy-done.4, f32[112,128]{1,0:T(8,128)S(1)} %get-tuple-element.225.across, ...), custom_call_target="tpu_custom_call", output_to_operand_aliasing={{}: (7, {})} | custom-call | flops 50331648 | bytes 12582912 | tf_op jit(solution)/shard_map/fluxes/pallas_call | solution.py:554
  79.4 1.0 collective-permute-start.22
  80.3 0.6 collective-permute-start.21
  81.0 2.6 %collective-permute-start.20 = (f32[16,128]{1,0:T(8,128)S(1)}, f32[16,128]{1,0:T(8,128)S(1)}, u32[]{:S(2)}, u32[]{:S(2)}) collective-permute-start(f32[16,128]{1,0:T(8,128)S(1)} %add_add_fusion.2), channel_id=1, source_target_pairs={{0,1},{1,0},{2,3},{3,2},{4,5},{5,4},{6,7},{7,6},{8,9},{9,8},{10,11... | collective-permute-start | bytes 24584 | tf_op jit(solution)/shard_map/ppermute | solution.py:625
  83.5 6.1 %fluxes.10.rest_0_ = f32[16,128,128]{2,1,0:T(8,128)} custom-call(s32[16]{0:T(128)S(1)} %copy-done.7, f32[16,128,128]{2,1,0:T(8,128)S(1)} %get-tuple-element.224.amounts, f32[16,128]{1,0:T(8,128)S(1)} %copy-done.2, f32[16,128]{1,0:T(8,128)S(1)} %copy-done.4, f32[112,128]{1,0:T(8,128)S(1)} %get-tuple-element.225.across, ...), custom_call_target="tpu_custom_call", output_to_operand_aliasing={{}: (7, {})} | custom-call | flops 50331648 | bytes 12582912 | tf_op jit(solution)/shard_map/fluxes/pallas_call | solution.py:554
  89.7 0.6 collective-permute-start.25
  90.3 2.7 %collective-permute-start.24 = (f32[16,128]{1,0:T(8,128)S(1)}, f32[16,128]{1,0:T(8,128)S(1)}, u32[]{:S(2)}, u32[]{:S(2)}) collective-permute-start(f32[16,128]{1,0:T(8,128)S(1)} %add_add_fusion.1), channel_id=1, source_target_pairs={{0,8},{1,9},{2,10},{3,11},{4,12},{5,13},{6,14},{7,15},{8,0},{9,1},... | collective-permute-start | bytes 24584 | tf_op jit(solution)/shard_map/ppermute | solution.py:625
  93.0 0.8 collective-permute-start.23
  93.8 8.6 %fluxes.11 = f32[16,128,128]{2,1,0:T(8,128)} custom-call(s32[16]{0:T(128)S(1)} %copy-done.7, f32[16,128,128]{2,1,0:T(8,128)S(1)} %get-tuple-element.224.amounts, f32[16,128]{1,0:T(8,128)S(1)} %copy-done.2, f32[16,128]{1,0:T(8,128)S(1)} %copy-done.4, f32[112,128]{1,0:T(8,128)S(1)} %get-tuple-element.225.across, ...), custom_call_target="tpu_custom_call", output_to_operand_aliasing={{}: (7, {})} | custom-call | flops 75497472 | bytes 18874368 | tf_op jit(solution)/shard_map/fluxes/pallas_call | solution.py:554
  102.5 4.0 %recombine.1 = (f32[16,128,128]{2,1,0:T(8,128)}, f32[16,128,128]{2,1,0:T(8,128)}, f32[8,128]{1,0:T(8,128)S(1)}) custom-call(f32[16,128]{1,0:T(8,128)S(1)} %add_add_fusion.moments, f32[16,128,128]{2,1,0:T(8,128)} %state.9, f32[6,28,128,128]{3,2,1,0:T(8,128)S(1)} %bitcast.3), custom_call_target="tpu_custom_call" | custom-call | flops 6291456 | bytes 9437184 | tf_op jit(solution)/shard_map/recombine/pallas_call | solution.py:452
  106.4 0.6 slice.145
  107.0 0.8 while.30
  (30 shorter events, 0.1 us)
Async XLA Ops:
  2.0 30.2 %collective-permute-start.12 = (f32[12,128,128]{2,1,0:T(8,128)S(1)}, f32[12,128,128]{2,1,0:T(8,128)S(1)}, u32[]{:S(2)}, u32[]{:S(2)}) collective-permute-start(f32[12,128,128]{2,1,0:T(8,128)S(1)} %get-tuple-element.222), channel_id=1, source_target_pairs={{0,1},{1,2},{2,3},{3,4},{4,5},{5,6},{6,7},{7,8},{8,9},{9,10},{10,1... | collective-permute-start | bytes 2359304 | tf_op jit(solution)/shard_map/ppermute | solution.py:639
  5.5 26.7 %collective-permute-start.13 = (f32[12,128,128]{2,1,0:T(8,128)S(1)}, f32[12,128,128]{2,1,0:T(8,128)S(1)}, u32[]{:S(2)}, u32[]{:S(2)}) collective-permute-start(f32[12,128,128]{2,1,0:T(8,128)S(1)} %get-tuple-element.223), channel_id=1, source_target_pairs={{1,0},{2,1},{3,2},{4,3},{5,4},{6,5},{7,6},{8,7},{9,8},{10,9},{11,1... | collective-permute-start | bytes 2359304 | tf_op jit(solution)/shard_map/ppermute | solution.py:640
  10.9 1.2 %copy-start = (f32[16,128,128]{2,1,0:T(8,128)S(1)}, f32[16,128,128]{2,1,0:T(8,128)}, u32[]{:S(2)}) copy-start(f32[16,128,128]{2,1,0:T(8,128)} %vapour.1) | copy-start | bytes 3145732
  12.1 0.7 copy-start.5
  16.6 0.7 copy-start.1
  17.3 0.7 copy-start.3
  18.0 0.7 copy-start.6
  18.6 18.4 %copy-start.4 = (f32[16,128]{1,0:T(8,128)S(1)}, f32[16,128]{1,0:T(8,128)}, u32[]{:S(2)}) copy-start(f32[16,128]{1,0:T(8,128)} %albedo.11) | copy-start | bytes 24580
  18.6 18.4 %copy-start.7 = (s32[16]{0:T(128)S(1)}, s32[16]{0:T(128)}, u32[]{:S(2)}) copy-start(s32[16]{0:T(128)} %mask.11) | copy-start | bytes 196
  35.2 30.2 %copy-start.2 = (f32[16,128]{1,0:T(8,128)S(1)}, f32[16,128]{1,0:T(8,128)}, u32[]{:S(2)}) copy-start(f32[16,128]{1,0:T(8,128)} %cosine.11) | copy-start | bytes 24580
  35.2 10.4 %collective-permute-start.15 = (f32[4,2,128,128]{3,2,1,0:T(8,128)S(1)}, f32[4,2,128,128]{3,2,1,0:T(8,128)S(1)}, u32[]{:S(2)}, u32[]{:S(2)}) collective-permute-start(f32[4,2,128,128]{3,2,1,0:T(8,128)S(1)} %edges.1.packed), channel_id=1, source_target_pairs={{0,16},{16,32},{32,48},{48,64},{64,80},{80,96},{96,112},{112,0},{1... | collective-permute-start | bytes 1572872 | tf_op jit(solution)/shard_map/ppermute | solution.py:647
  35.3 10.4 %collective-permute-start.14 = (f32[4,2,128,128]{3,2,1,0:T(8,128)S(1)}, f32[4,2,128,128]{3,2,1,0:T(8,128)S(1)}, u32[]{:S(2)}, u32[]{:S(2)}) collective-permute-start(f32[4,2,128,128]{3,2,1,0:T(8,128)S(1)} %edges.1.packed), channel_id=1, source_target_pairs={{0,112},{16,0},{32,16},{48,32},{64,48},{80,64},{96,80},{112,96},{1... | collective-permute-start | bytes 1572872 | tf_op jit(solution)/shard_map/ppermute | solution.py:646
  65.2 3.9 %collective-permute-start.16 = (f32[16,128]{1,0:T(8,128)S(1)}, f32[16,128]{1,0:T(8,128)S(1)}, u32[]{:S(2)}, u32[]{:S(2)}) collective-permute-start(f32[16,128]{1,0:T(8,128)S(1)} %get-tuple-element.237), channel_id=1, source_target_pairs={{0,16},{16,0},{32,48},{48,32},{64,80},{80,64},{96,112},{112,96},{1... | collective-permute-start | bytes 24584 | tf_op jit(solution)/shard_map/ppermute | solution.py:625
  69.1 10.2 %collective-permute-start.19 = (f32[16,128]{1,0:T(8,128)S(1)}, f32[16,128]{1,0:T(8,128)S(1)}, u32[]{:S(2)}, u32[]{:S(2)}) collective-permute-start(f32[16,128]{1,0:T(8,128)S(1)} %add.122), channel_id=1, source_target_pairs={{0,96},{16,112},{32,64},{48,80},{64,32},{80,48},{96,0},{112,16},{1... | collective-permute-start | bytes 24584 | tf_op jit(solution)/shard_map/ppermute | solution.py:625
  69.5 9.8 %collective-permute-start.18 = (f32[16,128]{1,0:T(8,128)S(1)}, f32[16,128]{1,0:T(8,128)S(1)}, u32[]{:S(2)}, u32[]{:S(2)}) collective-permute-start(f32[16,128]{1,0:T(8,128)S(1)} %add.122), channel_id=1, source_target_pairs={{0,64},{16,80},{32,96},{48,112},{64,0},{80,16},{96,32},{112,48},{1... | collective-permute-start | bytes 24584 | tf_op jit(solution)/shard_map/ppermute | solution.py:625
  69.5 9.8 %collective-permute-start.17 = (f32[16,128]{1,0:T(8,128)S(1)}, f32[16,128]{1,0:T(8,128)S(1)}, u32[]{:S(2)}, u32[]{:S(2)}) collective-permute-start(f32[16,128]{1,0:T(8,128)S(1)} %add.122), channel_id=1, source_target_pairs={{0,32},{16,48},{32,0},{48,16},{64,96},{80,112},{96,64},{112,80},{1... | collective-permute-start | bytes 24584 | tf_op jit(solution)/shard_map/ppermute | solution.py:625
  79.4 10.3 %collective-permute-start.22 = (f32[16,128]{1,0:T(8,128)S(1)}, f32[16,128]{1,0:T(8,128)S(1)}, u32[]{:S(2)}, u32[]{:S(2)}) collective-permute-start(f32[16,128]{1,0:T(8,128)S(1)} %add_add_fusion.2), channel_id=1, source_target_pairs={{0,3},{1,2},{2,1},{3,0},{4,7},{5,6},{6,5},{7,4},{8,11},{9,10},{10,... | collective-permute-start | bytes 24584 | tf_op jit(solution)/shard_map/ppermute | solution.py:625
  80.3 9.3 %collective-permute-start.21 = (f32[16,128]{1,0:T(8,128)S(1)}, f32[16,128]{1,0:T(8,128)S(1)}, u32[]{:S(2)}, u32[]{:S(2)}) collective-permute-start(f32[16,128]{1,0:T(8,128)S(1)} %add_add_fusion.2), channel_id=1, source_target_pairs={{0,2},{1,3},{2,0},{3,1},{4,6},{5,7},{6,4},{7,5},{8,10},{9,11},{10,... | collective-permute-start | bytes 24584 | tf_op jit(solution)/shard_map/ppermute | solution.py:625
  81.0 8.7 %collective-permute-start.20 = (f32[16,128]{1,0:T(8,128)S(1)}, f32[16,128]{1,0:T(8,128)S(1)}, u32[]{:S(2)}, u32[]{:S(2)}) collective-permute-start(f32[16,128]{1,0:T(8,128)S(1)} %add_add_fusion.2), channel_id=1, source_target_pairs={{0,1},{1,0},{2,3},{3,2},{4,5},{5,4},{6,7},{7,6},{8,9},{9,8},{10,11... | collective-permute-start | bytes 24584 | tf_op jit(solution)/shard_map/ppermute | solution.py:625
  89.7 12.8 %collective-permute-start.25 = (f32[16,128]{1,0:T(8,128)S(1)}, f32[16,128]{1,0:T(8,128)S(1)}, u32[]{:S(2)}, u32[]{:S(2)}) collective-permute-start(f32[16,128]{1,0:T(8,128)S(1)} %add_add_fusion.1), channel_id=1, source_target_pairs={{0,12},{1,13},{2,14},{3,15},{4,8},{5,9},{6,10},{7,11},{8,4},{9,5},... | collective-permute-start | bytes 24584 | tf_op jit(solution)/shard_map/ppermute | solution.py:625
  90.3 12.2 %collective-permute-start.24 = (f32[16,128]{1,0:T(8,128)S(1)}, f32[16,128]{1,0:T(8,128)S(1)}, u32[]{:S(2)}, u32[]{:S(2)}) collective-permute-start(f32[16,128]{1,0:T(8,128)S(1)} %add_add_fusion.1), channel_id=1, source_target_pairs={{0,8},{1,9},{2,10},{3,11},{4,12},{5,13},{6,14},{7,15},{8,0},{9,1},... | collective-permute-start | bytes 24584 | tf_op jit(solution)/shard_map/ppermute | solution.py:625
  93.0 9.4 %collective-permute-start.23 = (f32[16,128]{1,0:T(8,128)S(1)}, f32[16,128]{1,0:T(8,128)S(1)}, u32[]{:S(2)}, u32[]{:S(2)}) collective-permute-start(f32[16,128]{1,0:T(8,128)S(1)} %add_add_fusion.1), channel_id=1, source_target_pairs={{0,4},{1,5},{2,6},{3,7},{4,0},{5,1},{6,2},{7,3},{8,12},{9,13},{10,... | collective-permute-start | bytes 24584 | tf_op jit(solution)/shard_map/ppermute | solution.py:625
